TPU v7x, 128 devices: a whole 4x4x4 slice. The times are simulated.
128 devices in a mesh: seq: 16 (over y, x), exp: 8 (over z, core).
Axes of the slice: x: 4, y: 4, z: 4, core: 2. Of those that a mesh axis runs over, the one named last changes fastest.
Arguments:
- queries: bfloat16 [2048, 8192], P('seq', 'exp'), may hold values from -0.5 to 0.5
- keys: bfloat16 [2048, 8192], P('seq', 'exp'), may hold values from -0.5 to 0.5
- values: bfloat16 [2048, 8192], P('seq', 'exp'), may hold values from -6 to 6
- attn_grad: bfloat16 [2048, 8192], P('seq', 'exp'), may hold values from -6 to 6
- log_decay: float32 [2048, 64], P('seq', 'exp'), may hold values from -0.75 to 0, as said below
- moe_grad: bfloat16 [2048, 6144], P('seq', 'exp'), may hold values from -6 to 6
- gate_probs: bfloat16 [2048, 2], P('seq'), may hold values from 0.099609375 to 0.8984375
- expert_ids: int32 [2048, 2], P('seq'), may hold values from 0 to 7, all different within a row; in each aligned block of 128 rows (0 to 127, 128 to 255, ...) at most 48 rows name the same one
- hidden_acts: bfloat16 [8, 768, 9216], P('exp', None, 'seq'), may hold values from -0.3125 to 0.3125
- down_weight: bfloat16 [8, 9216, 6144], P('exp', 'seq'), may hold values from -0.0625 to 0.0625
Outputs:
- query_grad: bfloat16 [2048, 8192], P('seq', 'exp')
- key_grad: bfloat16 [2048, 8192], P('seq', 'exp')
- value_grad: bfloat16 [2048, 8192], P('seq', 'exp')
- hidden_grad: bfloat16 [8, 768, 9216], P('exp', None, 'seq')
- weight_grad: bfloat16 [8, 9216, 6144], P('exp', 'seq')
- gate_grad: float32 [2048, 2], P('seq')
Inputs may be any that keep to these rules, and one draw needn't show every extreme that they name: `expert_ids`: each row names 2 different experts. In the 128 rows of one index of seq no expert is named by more than 48 rows, and every draw has such a block where some expert is named by exactly 48 rows. `log_decay`: log decay of each head at each position; never positive.
All inputs are finite; a program needn't handle non-finite values.
Results may differ from a plain program's by a relative error of at most 0.005.
Values may be sent and summed in bfloat16 or wider, within the bound.
A program may use at most 128 MiB of HBM per device.

v0:
```python
import jax
import jax.numpy as jnp
from jax import lax
from jax.sharding import PartitionSpec as P

precise = lax.Precision.HIGHEST


def prefix(part, axis, combine, identity, reverse):
    count = lax.axis_size(axis)
    place = lax.axis_index(axis)
    ahead = count - 1 - place if reverse else place
    gathered = jax.tree.map(lambda a: lax.all_gather(a, axis), part)
    state = jax.tree.map(lambda a, e: jnp.zeros_like(a) + jnp.asarray(e, a.dtype), part, identity)

    def one(lap, state):
        source = count - 1 - lap if reverse else lap
        return combine(
            state, jax.tree.map(lambda a: lax.dynamic_index_in_dim(a, source, 0, False), gathered)
        )

    return lax.fori_loop(0, ahead, one, state)


def chain_combine(earlier, latter):
    return (jnp.exp(latter[1])[:, None, None] * earlier[0] + latter[0], earlier[1] + latter[1])


def on_device(
    queries,
    keys,
    values,
    attn_grad,
    log_decay,
    moe_grad,
    gate_probs,
    expert_ids,
    hidden_acts,
    down_weight,
):
    tok_count = queries.shape[0]
    head_count = log_decay.shape[1]
    head_width = queries.shape[1] // head_count
    shaped = (tok_count, head_count, head_width)
    query_f = queries.astype(jnp.float32).reshape(shaped)
    key_f = keys.astype(jnp.float32).reshape(shaped)
    value_f = values.astype(jnp.float32).reshape(shaped)
    grad_f = attn_grad.astype(jnp.float32).reshape(shaped)
    cumul = jnp.cumsum(log_decay, axis=0)
    total = cumul[-1]
    tail_w = jnp.exp(total[None, :] - cumul)
    lead_w = jnp.exp(cumul)
    state_kv = jnp.einsum("th,thi,thj->hij", tail_w, key_f, value_f, precision=precise)
    state_qg = jnp.einsum("th,thi,thj->hij", lead_w, query_f, grad_f, precision=precise)
    zero_state = jnp.zeros_like(state_kv)
    zero_gain = jnp.zeros_like(total)
    incoming = prefix((state_kv, total), "seq", chain_combine, (zero_state, zero_gain), False)[0]
    upcoming = prefix((state_qg, total), "seq", chain_combine, (zero_state, zero_gain), True)[0]
    causal = jnp.arange(tok_count)[:, None] >= jnp.arange(tok_count)[None, :]
    spread = cumul.T[:, :, None] - cumul.T[:, None, :]
    decay_mask = jnp.exp(jnp.where(causal[None], spread, -jnp.inf))
    grad_scores = jnp.einsum("thj,shj->hts", grad_f, value_f, precision=precise) * decay_mask
    qk_scores = jnp.einsum("thi,shi->hts", query_f, key_f, precision=precise) * decay_mask
    query_g = jnp.einsum("hts,shi->thi", grad_scores, key_f, precision=precise)
    query_g = query_g + lead_w[:, :, None] * jnp.einsum(
        "thj,hij->thi", grad_f, incoming, precision=precise
    )
    key_g = jnp.einsum("hts,thi->shi", grad_scores, query_f, precision=precise)
    key_g = key_g + tail_w[:, :, None] * jnp.einsum(
        "shj,hij->shi", value_f, upcoming, precision=precise
    )
    value_g = jnp.einsum("hts,thj->shj", qk_scores, grad_f, precision=precise)
    value_g = value_g + tail_w[:, :, None] * jnp.einsum(
        "shi,hij->shj", key_f, upcoming, precision=precise
    )
    flat_width = head_count * head_width
    query_grad = query_g.reshape(tok_count, flat_width).astype(jnp.bfloat16)
    key_grad = key_g.reshape(tok_count, flat_width).astype(jnp.bfloat16)
    value_grad = value_g.reshape(tok_count, flat_width).astype(jnp.bfloat16)
    expert_here = lax.axis_index("exp")
    cap_size = hidden_acts.shape[1] // lax.axis_size("seq")
    chosen_here = expert_ids == expert_here
    routed = jnp.any(chosen_here, axis=1)
    token_gate = jnp.sum(jnp.where(chosen_here, gate_probs.astype(jnp.float32), 0.0), axis=1)
    slot_rank = jnp.cumsum(routed.astype(jnp.int32)) - 1
    slot_ids = jnp.arange(cap_size, dtype=jnp.int32)
    selector = ((slot_rank[None, :] == slot_ids[:, None]) & routed[None, :]).astype(jnp.float32)
    slot_gate = jnp.dot(selector, token_gate, precision=precise).astype(jnp.bfloat16)
    whole_rows = lax.all_gather(moe_grad, "exp", axis=1, tiled=True)
    slot_rows = jnp.dot(
        selector.astype(jnp.bfloat16), whole_rows, preferred_element_type=jnp.float32
    ).astype(jnp.bfloat16)
    weight_here = down_weight[0]
    hidden_here = hidden_acts[0]
    piece_rows = lax.all_gather(slot_rows, "seq", axis=0, tiled=True)
    piece_gate = lax.all_gather(slot_gate, "seq", axis=0, tiled=True)
    back_rows = lax.dot_general(
        piece_rows, weight_here, (((1,), (1,)), ((), ())), preferred_element_type=jnp.float32
    )
    gate_col = piece_gate.astype(jnp.float32)[:, None]
    hidden_out = (gate_col * back_rows).astype(jnp.bfloat16)
    piece_parts = jnp.sum(back_rows * hidden_here.astype(jnp.float32), axis=1)
    slot_parts = piece_parts
    weighted = (gate_col * piece_rows.astype(jnp.float32)).astype(jnp.bfloat16)
    grad_sum = lax.dot_general(
        hidden_here, weighted, (((0,), (0,)), ((), ())), preferred_element_type=jnp.float32
    )
    grad_sum, hidden_out, slot_parts = (grad_sum, hidden_out, slot_parts)
    own_parts = lax.psum_scatter(slot_parts, "seq", scatter_dimension=0, tiled=True)
    per_token = jnp.dot(selector.T, own_parts, precision=precise)
    local_gate = jnp.where(chosen_here, per_token[:, None], 0.0)
    gate_grad = lax.psum(local_gate, "exp")
    return (
        query_grad,
        key_grad,
        value_grad,
        hidden_out[None],
        grad_sum.astype(jnp.bfloat16)[None],
        gate_grad,
    )


def solution(mesh):
    return jax.shard_map(
        on_device,
        mesh=mesh,
        in_specs=(
            P("seq", "exp"),
            P("seq", "exp"),
            P("seq", "exp"),
            P("seq", "exp"),
            P("seq", "exp"),
            P("seq", "exp"),
            P("seq", None),
            P("seq", None),
            P("exp", None, "seq"),
            P("exp", "seq", None),
        ),
        out_specs=(
            P("seq", "exp"),
            P("seq", "exp"),
            P("seq", "exp"),
            P("exp", None, "seq"),
            P("exp", "seq", None),
            P("seq", None),
        ),
        check_vma=False,
    )
```

profile of v0, /device:TPU:1, one launch (start us, length us, event | category | flops | bytes accessed | tf_op | source)
XLA Modules:
  0.0 343.7 jit_solution(9725436786065418335)
XLA Ops:
  7.2 0.0 copy-start
  7.2 0.0 copy-start.1
  7.2 0.0 all-gather.8.cloned.1.call-start
  7.2 0.7 all-gather.8.cloned.1.call-update
  7.9 0.0 all-gather.12.cloned.1.call-start
  8.0 0.8 copy.64
  8.8 1.1 copy.67
  9.9 0.2 reduce_window_sum.18
  10.1 0.0 copy-done
  10.2 1.2 fusion.21
  11.4 0.0 all-gather.12.cloned.1.call-update
  11.4 0.0 all-gather.14.cloned.1.call-start
  11.4 1.1 copy.93
  12.6 1.1 copy.74
  13.8 1.5 fusion.18
  15.2 0.0 all-gather.14.cloned.1.call-update
  15.3 0.0 all-gather.10.cloned.1.call-start
  15.3 0.7 select_reduce_fusion
  16.1 0.1 copy.83
  16.2 0.2 reduce-window.8
  16.4 0.1 add_reduce_fusion
  16.5 21.5 %all-gather.8.cloned.1.call-done = bf16[128,6144]{1,0:T(8,128)(2,1)} async-done(((bf16[128,768]{1,0:T(8,128)(2,1)}), bf16[128,6144]{1,0:T(8,128)(2,1)}) %all-gather.8.cloned.1.call-update) | async-done | bytes 1572880 | tf_op jit(solution)/shard_map/all_gather | solution.py:89
  37.9 2.6 convolution_convert_fusion
  40.5 0.0 all-gather.10.cloned.1.call-update
  40.6 0.6 fusion.44
  41.8 0.1 fusion.15
  41.9 0.2 dynamic-update-slice
  42.1 33.4 %all-reduce = bf16[768]{0:T(1024)(128)(2,1)S(1)} all-reduce(bf16[768]{0:T(1024)(128)(2,1)S(1)} %dynamic-update-slice), channel_id=1, replica_groups=mesh['seq'=16,'exp'=8] {'seq'}, use_global_device_ids=true, to_apply=%add | all-reduce | flops 768 | bytes 3072
  76.2 15.0 %all-gather.2 = f32[16,1,8]{2,1,0:T(1,128)S(1)} all-gather(f32[1,1,8]{2,1,0:T(1,128)S(1)} %get-tuple-element.211), channel_id=1, replica_groups=mesh['seq'=16,'exp'=8] {'seq'}, dimensions={0}, use_global_device_ids=true | all-gather | bytes 544 | tf_op jit(solution)/shard_map/all_gather | solution.py:13
  91.2 0.3 convolution_multiply_fusion.1
  91.5 0.3 convolution_multiply_fusion
  91.9 19.4 %all-gather.12.cloned.1.call-done = f32[128,128,128]{2,1,0:T(8,128)} async-done(((f32[8,128,128]{2,1,0:T(8,128)}), f32[128,128,128]{2,1,0:T(8,128)}) %all-gather.12.cloned.1.call-update) | async-done | bytes 8388624 | tf_op jit(solution)/shard_map/all_gather | solution.py:13
  111.3 0.4 fusion.7
  111.7 0.7 fusion.14
  112.4 0.8 copy.84
  113.2 70.5 %all-gather.14.cloned.1.call-done = f32[128,128,128]{2,1,0:T(8,128)} async-done(((f32[8,128,128]{2,1,0:T(8,128)}), f32[128,128,128]{2,1,0:T(8,128)}) %all-gather.14.cloned.1.call-update) | async-done | bytes 8388624 | tf_op jit(solution)/shard_map/all_gather | solution.py:13
  183.7 18.6 %while.27 = (s32[]{:T(128)}, f32[8,128,128]{2,1,0:T(8,128)S(1)}, s32[]{:T(128)}, f32[16,8]{1,0:T(8,128)S(1)}, f32[16,8,128,128]{3,2,1,0:T(8,128)}, /*index=5*/s32[]{:T(128)}, s32[]{:T(128)}, s32[]{:T(128)}, s32[]{:T(128)}) while((s32[]{:T(128)}, f32[8,128,128]{2,1,0:T(8,128)S(1)}, s32[]{:T(128)}, f32[16,8]{1,0:T(8,128)S(1)}, ...), condition=%wide.region_4.5_spmd, body=%wide.region_3.4_spmd.sunk | while | flops 262150 | bytes 1573115 | solution.py:22
  183.8 1.2 bitcast_add_fusion.5
  185.0 1.2 bitcast_add_fusion.5
  186.2 1.2 bitcast_add_fusion.5
  187.5 1.2 bitcast_add_fusion.5
  188.7 1.2 bitcast_add_fusion.5
  189.9 1.2 bitcast_add_fusion.5
  191.2 1.2 bitcast_add_fusion.5
  192.4 1.2 bitcast_add_fusion.5
  193.6 1.2 bitcast_add_fusion.5
  194.9 1.2 bitcast_add_fusion.5
  196.1 1.2 bitcast_add_fusion.5
  197.4 1.2 bitcast_add_fusion.5
  198.6 1.2 bitcast_add_fusion.5
  199.9 1.2 bitcast_add_fusion.5
  201.1 1.2 bitcast_add_fusion.5
  202.3 0.7 fusion.9
  203.0 0.4 fusion.13
  203.4 0.8 copy.85
  204.2 0.6 fusion.11
  204.8 0.4 fusion.12
  205.2 0.9 copy.86
  206.1 55.5 %all-gather.10.cloned.1.call-done = bf16[768,6144]{1,0:T(8,128)(2,1)} async-done(((bf16[48,6144]{1,0:T(8,128)(2,1)}), bf16[768,6144]{1,0:T(8,128)(2,1)}) %all-gather.10.cloned.1.call-update) | async-done | bytes 9437200 | tf_op jit(solution)/shard_map/all_gather | solution.py:95
  261.6 11.6 %multiply_reduce_fusion = (f32[768]{0:T(1024)S(1)}, bf16[1,768,576]{1,2,0:T(8,128)(2,1)}) fusion(bf16[1,768,576]{1,2,0:T(8,128)(2,1)} %param.22, f32[768]{0:T(1024)S(1)} %convert_element_type.83, bf16[768,6144]{1,0:T(8,128)(2,1)} %all-gather.10.cloned.1.call-done, bf16[1,576,6144]{2,1,0:T(8,128)(2,1)} %param.23), kind=kOutput, calls=%fused_computation.12 | convolution fusion | flops 5438028800 | bytes 18290688 | tf_op jit(solution)/shard_map/dot_general | solution.py:97
  273.2 31.2 %all-reduce.1 = f32[768]{0:T(1024)S(1)} all-reduce(f32[768]{0:T(1024)S(1)} %get-tuple-element.206), channel_id=4, replica_groups=mesh['seq'=16,'exp'=8] {'seq'}, use_global_device_ids=true, to_apply=%region_9.10.clone | all-reduce | flops 768 | bytes 6144
  304.3 0.2 convolution_bitcast_fusion.6
  304.5 20.6 %psum.7 = f32[128,2]{0,1:T(2,128)} all-reduce(f32[128,2]{0,1:T(2,128)S(1)} %broadcast_select_fusion), channel_id=1, replica_groups=mesh['seq'=16,'exp'=8] {'exp'}, use_global_device_ids=true, to_apply=%region_10.11 | all-reduce | flops 256 | bytes 2048 | tf_op jit(solution)/shard_map/psum | solution.py:112
  325.1 12.0 %fusion.3 = bf16[1,576,6144]{2,1,0:T(8,128)(2,1)} fusion(bf16[768,6144]{1,0:T(8,128)(2,1)} %all-gather.10.cloned.1.call-done, f32[768]{0:T(1024)S(1)} %convert_element_type.83, bf16[1,768,576]{1,2,0:T(8,128)(2,1)S(1)} %copy-done.2), kind=kOutput, calls=%fused_computation.8 | convolution fusion | flops 5453512704 | bytes 17402880 | tf_op jit(solution)/shard_map/dot_general | solution.py:105
  (32 shorter events, 0.5 us)
Async XLA Ops:
  7.2 3.0 copy-start
  7.2 33.4 %copy-start.1 = (u32[128]{0:T(128)S(1)}, u32[128]{0:T(128)}, u32[]{:S(2)}) copy-start(u32[128]{0:T(128)} %constant.81) | copy-start | bytes 1540
  7.2 30.7 %all-gather.8.cloned.1.call-start = ((), (), s32[]{:S(2)}) async-start(), calls=%async_computation | async-start | bytes 1769472 | tf_op jit(solution)/shard_map/all_gather | solution.py:89
  7.9 103.3 %all-gather.12.cloned.1.call-start = ((), (), s32[]{:S(2)}) async-start(), calls=%async_computation.2 | async-start | bytes 8912896 | tf_op jit(solution)/shard_map/all_gather | solution.py:13
  11.4 172.3 %all-gather.14.cloned.1.call-start = ((), (), s32[]{:S(2)}) async-start(), calls=%async_computation.3 | async-start | bytes 8912896 | tf_op jit(solution)/shard_map/all_gather | solution.py:13
  15.3 246.3 %all-gather.10.cloned.1.call-start = ((), (), s32[]{:S(2)}) async-start(), calls=%async_computation.1 | async-start | bytes 10027008 | tf_op jit(solution)/shard_map/all_gather | solution.py:95
  206.1 119.0 %copy-start.2 = (bf16[1,768,576]{1,2,0:T(8,128)(2,1)S(1)}, bf16[1,768,576]{1,2,0:T(8,128)(2,1)}, u32[]{:S(2)}) copy-start(bf16[1,768,576]{1,2,0:T(8,128)(2,1)} %param.22) | copy-start | bytes 2654212
Sparse Core Ops, SparseCore 0:
  9.7 28.1 all-gather.7
  40.6 70.5 all-gather.11
  113.4 70.2 all-gather.13
  186.2 75.2 all-gather.9
where the time goes:
time: 345 us; the launch traced here: 344 us
  waiting for transfers between devices  168 us (49%)
  blocking collectives  100 us (29%)
  matrix products  33 us (10%)
  other arithmetic  19.2 us (6%)
  between operations  15.2 us (4%)
  local copies, waits for them, and re-layouts  8.11 us (2%)
    all_gather x2, waiting for transfers between devices, prefix(): gathered = jax.tree.map(lambda a: lax.all_gather(a, axis), part)  89.8 us
    unnamed x2, blocking collectives  64.5 us
    all_gather x1, waiting for transfers between devices, on_device(): piece_rows = lax.all_gather(slot_rows, 'seq', axis=0, tiled=True)  55.5 us
    all_gather x1, waiting for transfers between devices, on_device(): whole_rows = lax.all_gather(moe_grad, 'exp', axis=1, tiled=True)  21.5 us
    psum x1, blocking collectives, on_device(): gate_grad = lax.psum(local_gate, 'exp')  20.6 us
    add x15, other arithmetic, chain_combine(): jnp.exp(latter[1])[:, None, None] * earlier[0] + latter[0]  17.9 us
    all_gather x1, blocking collectives, prefix(): gathered = jax.tree.map(lambda a: lax.all_gather(a, axis), part)  15 us
    dot_general x1, matrix products, on_device(): lax.dot_general(hidden_here, weighted, (((0,), (0,)), ((), ())), preferre...  12 us
  transfers between devices with their start and end apart: 4, of which 4 were waited for; matrix products, arithmetic and copies ran while one was open for 11% of the time, Pallas kernels for 0%

commit v1 on v0

v1 whole, which is shorter than its diff:
```python
import functools

import jax
import jax.numpy as jnp
from jax import lax
from jax.experimental import pallas as pl
from jax.experimental.pallas import tpu as pltpu
from jax.sharding import PartitionSpec as P

MESH = pl.DeviceIdType.MESH
BF, F32, I32 = jnp.bfloat16, jnp.float32, jnp.int32
NX, NY = 4, 4

OFFS = [
    (0, 0), (-1, 0), (1, 0), (0, -1), (0, 1), (2, 0), (0, 2), (-1, -1),
    (1, -1), (-1, 1), (1, 1), (2, -1), (2, 1), (-1, 2), (1, 2), (2, 2),
]
SLOT = {off: i for i, off in enumerate(OFFS)}
DIRS = {"xp": (1, 0), "xm": (-1, 0), "yp": (0, 1), "ym": (0, -1)}
H1, H2, H1b, H1a, H2a, H2b = (0, 2), (2, 4), (0, 1), (1, 2), (2, 3), (3, 4)

START = [
    ("xp", (0, 0), H1), ("xm", (0, 0), H1), ("yp", (0, 0), H2), ("ym", (0, 0), H2),
    ("xp", (0, 0), H2), ("xm", (0, 0), H2), ("yp", (0, 0), H1), ("ym", (0, 0), H1),
]
ROUND1 = [
    ([("xp", (0, 0), H1)], [("xp", (-1, 0), H1a), ("yp", (-1, 0), H1), ("ym", (-1, 0), H1)]),
    ([("xm", (0, 0), H1)], [("xm", (1, 0), H1b), ("yp", (1, 0), H1), ("ym", (1, 0), H1)]),
    ([("yp", (0, 0), H2)], [("yp", (0, -1), H2a), ("xp", (0, -1), H2), ("xm", (0, -1), H2)]),
    ([("ym", (0, 0), H2)], [("ym", (0, 1), H2b), ("xp", (0, 1), H2), ("xm", (0, 1), H2)]),
    ([("xp", (0, 0), H2)], [("xp", (-1, 0), H2a)]),
    ([("xm", (0, 0), H2)], [("xm", (1, 0), H2b)]),
    ([("yp", (0, 0), H1)], [("yp", (0, -1), H1a)]),
    ([("ym", (0, 0), H1)], [("ym", (0, 1), H1b)]),
]
ROUND2 = [
    ([("xp", (-1, 0), H1a), ("xm", (1, 0), H1b)], [("yp", (2, 0), H1), ("ym", (2, 0), H1)]),
    ([("yp", (0, -1), H2a), ("ym", (0, 1), H2b)], [("xp", (0, 2), H2), ("xm", (0, 2), H2)]),
    ([("xp", (0, -1), H2)], [("xp", (-1, -1), H2a)]),
    ([("xm", (0, -1), H2)], [("xm", (1, -1), H2b)]),
    ([("yp", (-1, 0), H1)], [("yp", (-1, -1), H1a)]),
    ([("ym", (-1, 0), H1)], [("ym", (-1, 1), H1b)]),
    ([("xp", (0, 1), H2)], [("xp", (-1, 1), H2a)]),
    ([("xm", (0, 1), H2)], [("xm", (1, 1), H2b)]),
    ([("yp", (1, 0), H1)], [("yp", (1, -1), H1a)]),
    ([("ym", (1, 0), H1)], [("ym", (1, 1), H1b)]),
    ([("xp", (-1, 0), H2a), ("xm", (1, 0), H2b), ("yp", (0, -1), H1a), ("ym", (0, 1), H1b)], []),
]
ROUND3 = [
    ([("yp", (2, 0), H1)], [("yp", (2, -1), H1a)]),
    ([("ym", (2, 0), H1)], [("ym", (2, 1), H1b)]),
    ([("xp", (0, 2), H2)], [("xp", (-1, 2), H2a)]),
    ([("xm", (0, 2), H2)], [("xm", (1, 2), H2b)]),
]
ROUND4 = [
    ([("xp", (-1, -1), H2a), ("xp", (-1, 1), H2a), ("xm", (1, -1), H2b), ("xm", (1, 1), H2b)], []),
    ([("yp", (-1, -1), H1a), ("yp", (1, -1), H1a), ("ym", (-1, 1), H1b), ("ym", (1, 1), H1b)], []),
    ([("yp", (2, -1), H1a), ("ym", (2, 1), H1b), ("xp", (-1, 2), H2a), ("xm", (1, 2), H2b)], []),
]
MSGS = START + [m for r in (ROUND1, ROUND2, ROUND3) for _, sends in r for m in sends]
INDEX = {m: i for i, m in enumerate(MSGS)}


def wrap(a, d):
    return tuple((p - q + 1) % 4 - 1 for p, q in zip(a, d))


def nn(a, b):
    return jnp.dot(a, b, preferred_element_type=F32)


def nt(a, b):
    return lax.dot_general(a, b, (((1,), (1,)), ((), ())), preferred_element_type=F32)


def iota(shape, axis):
    return lax.broadcasted_iota(I32, shape, axis)


def to_row(col, rows):
    eye = iota((rows, 128), 0) == iota((rows, 128), 1)
    return jnp.sum(jnp.where(eye, jnp.broadcast_to(col, (rows, 128)), 0.0), axis=0, keepdims=True)


def to_col(row):
    eye = iota((128, 128), 0) == iota((128, 128), 1)
    return jnp.sum(jnp.where(eye, jnp.broadcast_to(row, (128, 128)), 0.0), axis=1, keepdims=True)


def kernel(
    q_hbm, k_hbm, v_hbm, g_hbm, moe_hbm, hid_hbm, w_hbm, decay, gates, ids,
    qg_hbm, kg_hbm, vg_hbm, ho_hbm, wg_hbm, gate_out,
    qb, kb, vb, gb, moe, hid, hid_t, w, x, pack, sel, back, acc, wg, ho, parts_c,
    parts_s, parts_r, tok_s, tok_r, st_s, st_r, res_s, res_r, cum, qo, ko, vo,
    load_sem, out_sem, z_send, z_recv, a_send, a_recv, b_send, b_recv,
    x_send, x_recv, p_send, p_recv, t_send, t_recv,
):
    n_seq, n_exp = lax.axis_size("seq"), lax.axis_size("exp")
    me, e = lax.axis_index("seq"), lax.axis_index("exp")
    my_y, my_x = me // NX, me % NX
    cap = x.shape[0] // n_seq
    feat = moe.shape[1]
    width = w.shape[1]
    heads = decay.shape[1]
    quarter = width // 4

    def seq_at(off):
        return ((my_y + off[1] + NY) % NY) * NX + (my_x + off[0] + NX) % NX

    def remote(src, dst, ss, rs, where):
        return pltpu.make_async_remote_copy(
            src_ref=src, dst_ref=dst, send_sem=ss, recv_sem=rs,
            device_id=where, device_id_type=MESH,
        )

    loads = [(moe_hbm, moe), (q_hbm, qb), (k_hbm, kb), (v_hbm, vb), (g_hbm, gb)]
    loads = [pltpu.make_async_copy(a, b, load_sem.at[i]) for i, (a, b) in enumerate(loads)]
    n_load = len(loads)
    hid_loads = []
    for i, off in enumerate(OFFS):
        start = pl.multiple_of(seq_at(off) * cap, 16)
        hid_loads.append(pltpu.make_async_copy(
            hid_hbm.at[pl.ds(start, cap)], hid.at[pl.ds(i * cap, cap)], load_sem.at[n_load + i]))
    w_load = pltpu.make_async_copy(w_hbm, w, load_sem.at[n_load + n_seq])
    for c in loads + hid_loads + [w_load]:
        c.start()

    barrier = pltpu.get_barrier_semaphore()
    for off in range(1, n_seq):
        pl.semaphore_signal(barrier, inc=1, device_id={"seq": (me + off) % n_seq}, device_id_type=MESH)
    for off in range(1, n_exp):
        pl.semaphore_signal(barrier, inc=1, device_id={"exp": (e + off) % n_exp}, device_id_type=MESH)

    ids_f = ids[...].astype(F32)
    gates_f = gates[...].astype(F32)
    e_f = e.astype(F32)
    id_rows = [to_row(ids_f[:, k:k + 1], 128) for k in range(2)]
    expert = iota((n_exp, 128), 0).astype(F32)
    routed = jnp.where((expert == id_rows[0]) | (expert == id_rows[1]), 1.0, 0.0)
    upto = jnp.where(iota((128, 128), 0) <= iota((128, 128), 1), 1.0, 0.0).astype(BF)
    rank = nn(routed.astype(BF), upto) - 1.0
    rank = jnp.where(routed > 0.0, rank, -1.0)
    slot_no = iota((cap, 128), 0).astype(F32)
    loads[0].wait()
    for i in range(n_exp):
        chosen = jnp.where(rank[i:i + 1, :] == slot_no, 1.0, 0.0)
        pack[pl.ds(i * cap, cap), :] = nn(chosen.astype(BF), moe[...]).astype(BF)
    own_rank = jnp.max(jnp.where(expert == e_f, rank, -1.0), axis=0, keepdims=True)
    own = jnp.where(own_rank == slot_no, 1.0, 0.0)
    sel[...] = own
    tok_gate = sum(jnp.where(ids_f[:, k:k + 1] == e_f, gates_f[:, k:k + 1], 0.0) for k in range(2))
    slot_gate = jnp.sum(own * to_row(tok_gate, 128), axis=1, keepdims=True)
    x[0:cap, width:] = jnp.broadcast_to(slot_gate, (cap, 128)).astype(BF)

    pl.semaphore_wait(barrier, n_seq - 1 + n_exp - 1)

    col_here = pl.ds(pl.multiple_of(e * feat, 128), feat)
    z_copies = []
    for off in range(1, n_exp):
        peer = (e + off) % n_exp
        z_copies.append(remote(
            pack.at[pl.ds(pl.multiple_of(peer * cap, 16), cap)], x.at[pl.ds(0, cap), col_here],
            z_send.at[off], z_recv.at[off], {"exp": peer}))
        z_copies[-1].start()
    x[0:cap, col_here] = pack[pl.ds(pl.multiple_of(e * cap, 16), cap), :]

    cum[...] = jnp.dot(
        jnp.where(iota((128, 128), 0) >= iota((128, 128), 1), 1.0, 0.0), decay[...],
        preferred_element_type=F32, precision=lax.Precision.HIGHEST)
    for c in loads[1:]:
        c.wait()

    def head_terms(h):
        here = iota((128, heads), 1) == h
        col = jnp.sum(jnp.where(here, cum[...], 0.0), axis=1, keepdims=True)
        return col, col[127:128, :]

    def local_state(h, carry):
        col, total = head_terms(h)
        cols = pl.ds(pl.multiple_of(h * 128, 128), 128)
        kw = (kb[:, cols].astype(F32) * jnp.exp(total - col)).T.astype(BF)
        qw = (qb[:, cols].astype(F32) * jnp.exp(col)).T.astype(BF)
        kv = nn(kw, vb[:, cols]).astype(BF)
        qg = nn(qw, gb[:, cols]).astype(BF)
        gain = jnp.broadcast_to(jnp.exp(total), (16, 128))
        hi = gain.astype(BF).astype(F32)
        mid = (gain - hi).astype(BF).astype(F32)
        low = gain - hi - mid
        row = iota((16, 128), 0)
        three = jnp.where(row == 0, hi, jnp.where(row == 1, mid, jnp.where(row == 2, low, 0.0))).astype(BF)
        for p in range(2):
            st_s[2 * h + p, 0:64, :] = kv[64 * p:64 * p + 64, :]
            st_s[2 * h + p, 64:128, :] = qg[64 * p:64 * p + 64, :]
            st_s[2 * h + p, 128:144, :] = three
        return carry

    lax.fori_loop(0, heads, local_state, 0)
    a_copies = []
    for off in range(1, n_seq):
        peer = (me + off) % n_seq
        a_copies.append(remote(st_s.at[peer], st_r.at[me], a_send.at[off], a_recv.at[off], {"seq": peer}))
        a_copies[-1].start()
    st_r[me] = st_s[me]

    def span(q):
        stop = width + 128 if q[1] == 4 else q[1] * quarter
        return pl.ds(q[0] * quarter, stop - q[0] * quarter)

    def message(m):
        d, off, q = m
        i = INDEX[m]
        src = x.at[pl.ds(SLOT[off] * cap, cap), span(q)]
        dst = x.at[pl.ds(SLOT[wrap(off, DIRS[d])] * cap, cap), span(q)]
        return remote(src, dst, x_send.at[i], x_recv.at[i], {"seq": seq_at(DIRS[d])})

    def go(steps):
        for waits, sends in steps:
            for m in waits:
                message(m).wait_recv()
            for m in sends:
                message(m).start()

    for c in z_copies:
        c.wait_recv()
    go([([], START)])

    for c in a_copies:
        c.wait_recv()

    def gain_of(b):
        g3 = st_r[b, 128:144, :].astype(F32)
        return g3[0:1, :] + g3[1:2, :] + g3[2:3, :]

    def scan_up(b, state):
        res_s[b, 0:64, :] = state.astype(BF)
        return gain_of(b) * state + st_r[b, 0:64, :].astype(F32)

    def scan_down(i, state):
        b = n_seq - 1 - i
        res_s[b, 64:128, :] = state.astype(BF)
        return gain_of(b) * state + st_r[b, 64:128, :].astype(F32)

    zero = jnp.zeros((64, 128), F32)
    lax.fori_loop(0, n_seq, scan_up, zero)
    lax.fori_loop(0, n_seq, scan_down, zero)
    b_copies = []
    for off in range(1, n_seq):
        peer = (me + off) % n_seq
        b_copies.append(remote(res_s.at[peer], res_r.at[me], b_send.at[off], b_recv.at[off], {"seq": peer}))
        b_copies[-1].start()
    res_r[me] = res_s[me]

    for c in hid_loads:
        c.wait()

    def turn(i, carry):
        rows = pl.ds(pl.multiple_of(i * 128, 128), 128)
        hid_t[:, rows] = hid[rows, :].astype(F32).T.astype(BF)
        return carry

    lax.fori_loop(0, hid.shape[0] // 128, turn, 0)

    go(ROUND1)

    for c in b_copies:
        c.wait_recv()

    def finish_head(h, carry):
        col, total = head_terms(h)
        cols = pl.ds(pl.multiple_of(h * 128, 128), 128)
        q, k, v, g = qb[:, cols], kb[:, cols], vb[:, cols], gb[:, cols]
        two = res_r[pl.ds(2 * h, 2)]
        inc = two[:, 0:64, :].reshape(128, 128)
        upc = two[:, 64:128, :].reshape(128, 128)
        lead, tail = jnp.exp(col), jnp.exp(total - col)
        spread = jnp.broadcast_to(col, (128, 128)) - to_row(col, 128)
        causal = iota((128, 128), 0) >= iota((128, 128), 1)
        mask = jnp.exp(jnp.where(causal, spread, -jnp.inf))
        gs = nt(g, v) * mask
        qk = nt(q, k) * mask
        qo[:, cols] = (nn(gs.astype(BF), k) + lead * nt(g, inc)).astype(BF)
        ko[:, cols] = (nn(gs.T.astype(BF), q) + tail * nt(v, upc)).astype(BF)
        vo[:, cols] = (nn(qk.T.astype(BF), g) + tail * nn(k, upc)).astype(BF)
        return carry

    lax.fori_loop(0, heads, finish_head, 0)
    outs = [(qo, qg_hbm), (ko, kg_hbm), (vo, vg_hbm)]
    outs = [pltpu.make_async_copy(a, b, out_sem.at[i]) for i, (a, b) in enumerate(outs)]
    for c in outs:
        c.start()

    go(ROUND2)

    chunk = 512
    chunks = width // chunk
    n_rows = x.shape[0]
    cut = 512

    def product(start, count):
        rows = pl.ds(start, count)
        back[rows, :] = jnp.zeros((count, back.shape[1]), F32)

        def one(i, carry):
            cols = pl.ds(pl.multiple_of(i * chunk, chunk), chunk)
            back[rows, :] += nt(x[rows, cols], w[:, cols])
            return carry

        lax.fori_loop(0, chunks, one, 0)

        def after(i, carry):
            part = pl.ds(pl.multiple_of(start + i * 64, 64), 64)
            b = back[part, :]
            gate = x[part, width:][:, 0:1].astype(F32)
            ho[part, :] = (gate * b).astype(BF)
            total = jnp.sum(b * hid[part, :].astype(F32), axis=1, keepdims=True)
            parts_c[part, :] = jnp.broadcast_to(total, (64, 128))
            return carry

        lax.fori_loop(0, count // 64, after, 0)

    def scaled(start, count, cols):
        rows = pl.ds(start, count)
        gate = x[rows, width:]
        return x[rows, cols] * jnp.concatenate([gate] * (chunk // 128), axis=1)

    p_copies, ho_copies = [], []

    def hand_out(first, last):
        for i in range(first, last):
            rows = pl.ds(i * cap, cap)
            parts_s[i] = jnp.broadcast_to(to_row(parts_c[rows, :][:, 0:1], cap), (8, 128))
            owner = seq_at(OFFS[i])
            c = pltpu.make_async_copy(
                ho.at[rows], ho_hbm.at[pl.ds(pl.multiple_of(owner * cap, 16), cap)], out_sem.at[3 + i])
            c.start()
            ho_copies.append(c)
            if i > 0:
                c = remote(parts_s.at[i], parts_r.at[i], p_send.at[i], p_recv.at[i], {"seq": owner})
                c.start()
                p_copies.append(c)

    w_load.wait()
    product(0, cut)
    go(ROUND3)
    hand_out(0, cut // cap)

    def first_grad(i, carry):
        cols = pl.ds(pl.multiple_of(i * chunk, chunk), chunk)
        acc[:, cols] = nn(hid_t[:, 0:cut], scaled(0, cut, cols))
        return carry

    lax.fori_loop(0, chunks, first_grad, 0)
    go(ROUND4)
    product(cut, n_rows - cut)
    hand_out(cut // cap, n_seq)

    def wg_copy(i):
        cols = pl.ds(pl.multiple_of(i * chunk, chunk), chunk)
        return pltpu.make_async_copy(wg.at[:, cols], wg_hbm.at[:, cols], out_sem.at[3 + n_seq + i])

    def last_grad(i, carry):
        cols = pl.ds(pl.multiple_of(i * chunk, chunk), chunk)
        wg[:, cols] = (acc[:, cols] + nn(hid_t[:, cut:], scaled(cut, n_rows - cut, cols))).astype(BF)
        wg_copy(i).start()
        return carry

    lax.fori_loop(0, chunks, last_grad, 0)

    total = parts_s[0]
    for i, c in enumerate(p_copies):
        c.wait_recv()
        total = total + parts_r[i + 1]
    per_tok = jnp.sum(sel[...] * to_col(total[0:1, :])[0:cap, :], axis=0, keepdims=True)
    tok_s[...] = jnp.broadcast_to(per_tok, (8, 128))
    t_copies = []
    for off in range(1, n_exp):
        peer = (e + off) % n_exp
        t_copies.append(remote(tok_s, tok_r.at[e], t_send.at[off], t_recv.at[off], {"exp": peer}))
        t_copies[-1].start()
    tok_r[e] = tok_s[...]
    for c in t_copies:
        c.wait_recv()
    by_expert = [to_col(tok_r[i, 0:1, :]) for i in range(n_exp)]
    result = []
    for k in range(2):
        result.append(sum(jnp.where(ids_f[:, k:k + 1] == float(i), by_expert[i], 0.0) for i in range(n_exp)))
    gate_out[...] = jnp.where(iota((128, 2), 1) == 0, result[0], result[1])

    for c in z_copies + a_copies + b_copies + p_copies + t_copies:
        c.wait_send()
    for m in MSGS:
        message(m).wait_send()
    for c in outs + ho_copies:
        c.wait()
    for i in range(chunks):
        wg_copy(i).wait()


def on_device(
    queries, keys, values, attn_grad, log_decay, moe_grad, gate_probs, expert_ids, hidden_acts, down_weight
):
    n_seq, n_exp = lax.axis_size("seq"), lax.axis_size("exp")
    _, slots, units = hidden_acts.shape
    width = down_weight.shape[2]
    toks, flat = queries.shape
    feat = moe_grad.shape[1]
    hbm = pl.BlockSpec(memory_space=pl.ANY)
    vmem = pl.BlockSpec(memory_space=pltpu.VMEM)
    dma = pltpu.SemaphoreType.DMA
    V = pltpu.VMEM
    wide = V((toks, flat), BF)
    out = pl.pallas_call(
        kernel,
        out_shape=(
            jax.ShapeDtypeStruct((toks, flat), BF),
            jax.ShapeDtypeStruct((toks, flat), BF),
            jax.ShapeDtypeStruct((toks, flat), BF),
            jax.ShapeDtypeStruct((slots, units), BF),
            jax.ShapeDtypeStruct((units, width), BF),
            jax.ShapeDtypeStruct(gate_probs.shape, F32),
        ),
        in_specs=[hbm] * 7 + [vmem] * 3,
        out_specs=(hbm,) * 5 + (vmem,),
        scratch_shapes=[
            wide, wide, wide, wide, V((toks, feat), BF),
            V((slots, units), BF), V((units, slots), BF), V((units, width), BF),
            V((slots, width + 128), BF), V((n_exp * slots // n_seq, feat), BF),
            V((slots // n_seq, 128), F32), V((slots, units), F32), V((units, width), F32),
            V((units, width), BF), V((slots, units), BF), V((slots, 128), F32),
            V((n_seq, 8, 128), F32), V((n_seq, 8, 128), F32),
            V((8, 128), F32), V((n_exp, 8, 128), F32),
            V((n_seq, 144, 128), BF), V((n_seq, 144, 128), BF),
            V((n_seq, 128, 128), BF), V((n_seq, 128, 128), BF),
            V(log_decay.shape, F32), wide, wide, wide,
            dma((5 + n_seq + 1,)), dma((3 + n_seq + width // 512,)),
            dma((n_exp,)), dma((n_exp,)), dma((n_seq,)), dma((n_seq,)), dma((n_seq,)), dma((n_seq,)),
            dma((len(MSGS),)), dma((len(MSGS),)), dma((n_seq,)), dma((n_seq,)), dma((n_exp,)), dma((n_exp,)),
        ],
        compiler_params=pltpu.CompilerParams(
            collective_id=0, has_side_effects=True, vmem_limit_bytes=60 * 1024 * 1024
        ),
    )(
        queries, keys, values, attn_grad, moe_grad, hidden_acts[0], down_weight[0],
        log_decay, gate_probs, expert_ids,
    )
    return (*out[:3], out[3][None], out[4][None], out[5])


def solution(mesh):
    return jax.shard_map(
        on_device,
        mesh=mesh,
        in_specs=(
            P("seq", "exp"),
            P("seq", "exp"),
            P("seq", "exp"),
            P("seq", "exp"),
            P("seq", "exp"),
            P("seq", "exp"),
            P("seq", None),
            P("seq", None),
            P("exp", None, "seq"),
            P("exp", "seq", None),
        ),
        out_specs=(
            P("seq", "exp"),
            P("seq", "exp"),
            P("seq", "exp"),
            P("exp", None, "seq"),
            P("exp", "seq", None),
            P("seq", None),
        ),
        check_vma=False,
    )
```

time: 345 us -> 116 us (0.34)
  waiting for transfers between devices: 168 us -> 0 us
  blocking collectives: 100 us -> 0 us
  Pallas kernels: 0 us -> 93.3 us
  matrix products: 33 us -> 0 us
  other arithmetic: 19.2 us -> 0 us
  between operations: 15.2 us -> 0.64 us
  local copies, waits for them, and re-layouts: 8.11 us -> 21.9 us
    all_gather x4 -> x0, waiting for transfers between devices: 167 us -> none  [the longest x2 89.8 us: prefix(): gathered = jax.tree.map(lambda a: lax.all_gather(a, axis), part)]
    pallas_call x0 -> x1, Pallas kernels: none -> 93.3 us  [on_device(): pl.pallas_call(kernel, out_shape=(jax.ShapeDtypeStruct((toks, flat), BF),...]
    unnamed x2 -> x0, blocking collectives: 64.5 us -> none
    dot_general x15 -> x0, matrix products: 33 us -> none  [the longest x1 12 us: on_device(): lax.dot_general(hidden_here, weighted, (((0,), (0,)), ((), ())), preferre...]
    psum x1 -> x0, blocking collectives: 20.6 us -> none  [on_device(): gate_grad = lax.psum(local_gate, 'exp')]
    add x15 -> x0, other arithmetic: 17.9 us -> none  [chain_combine(): jnp.exp(latter[1])[:, None, None] * earlier[0] + latter[0]]
    unnamed x15 -> x10, local copies, waits for them, and re-layouts: 6.47 us -> 21.9 us
    all_gather x1 -> x0, blocking collectives: 15 us -> none  [prefix(): gathered = jax.tree.map(lambda a: lax.all_gather(a, axis), part)]
  transfers between devices with their start and end apart: 4 -> 0, of which waited for: 4 -> 0; matrix products, arithmetic and copies ran while one was open for 11% -> 0% of each run, Pallas kernels for 0% -> 0%
where the time goes in v1:
time: 116 us
  Pallas kernels  93.3 us (80%)
  local copies, waits for them, and re-layouts  21.9 us (19%)
    pallas_call x1, Pallas kernels, on_device(): pl.pallas_call(kernel, out_shape=(jax.ShapeDtypeStruct((toks, flat), BF),...  93.3 us
    unnamed x10, local copies, waits for them, and re-layouts  21.9 us

profile of v1, /device:TPU:1, one launch (start us, length us, event | category | flops | bytes accessed | tf_op | source)
XLA Modules:
  0.0 115.9 jit_solution(12053820759259089694)
XLA Ops:
  0.6 1.4 %copy.18.gates = bf16[128,2]{1,0:T(8,128)(2,1)} copy(bf16[128,2]{0,1:T(2,128)(2,1)} %param.16) | data formatting | bytes 1024 | tf_op args[6]
  2.0 1.4 %copy.17.decay = f32[128,8]{1,0:T(8,128)} copy(f32[128,8]{0,1:T(8,128)} %param.14) | data formatting | bytes 8192 | tf_op args[4]
  3.4 1.4 %copy.19.ids = s32[128,2]{1,0:T(8,128)} copy(s32[128,2]{0,1:T(2,128)} %param.17) | data formatting | bytes 2048 | tf_op args[7]
  4.8 2.2 %copy.16 = bf16[1,768,576]{2,1,0:T(8,128)(2,1)} copy(bf16[1,768,576]{1,2,0:T(8,128)(2,1)} %param.18) | data formatting | bytes 1769472 | tf_op args[8]
  7.1 93.3 %shard_map.145 = (bf16[128,1024]{1,0:T(8,128)(2,1)}, bf16[128,1024]{1,0:T(8,128)(2,1)}, bf16[128,1024]{1,0:T(8,128)(2,1)}, bf16[768,576]{1,0:T(8,128)(2,1)}, bf1...) custom-call(bf16[128,1024]{1,0:T(8,128)(2,1)} %q_hbm.1, bf16[128,1024]{1,0:T(8,128)(2,1)} %k_hbm.1, bf16[128,1024]{1,0:T(8,128)(2,1)} %v_hbm.1, ...), custom_call_target="tpu_custom_call" | custom-call | tf_op jit(solution)/shard_map/pallas_call | solution.py:412
  100.4 1.5 %copy.21 = f32[128,2]{0,1:T(2,128)} copy(f32[128,2]{1,0:T(8,128)} %get-tuple-element.23) | data formatting | bytes 2048
  101.8 2.2 %copy.20 = bf16[1,768,576]{1,2,0:T(8,128)(2,1)} copy(bf16[1,768,576]{2,1,0:T(8,128)(2,1)} %bitcast.7) | data formatting | bytes 1769472
  104.0 1.7 %copy.26 = bf16[128,1024]{1,0:T(8,128)(2,1)} copy(bf16[128,1024]{1,0:T(8,128)(2,1)} %get-tuple-element.30) | data formatting | bytes 524288
  105.7 1.7 %copy.27 = bf16[128,1024]{1,0:T(8,128)(2,1)} copy(bf16[128,1024]{1,0:T(8,128)(2,1)} %get-tuple-element.31) | data formatting | bytes 524288
  107.4 1.7 %copy.28 = bf16[128,1024]{1,0:T(8,128)(2,1)} copy(bf16[128,1024]{1,0:T(8,128)(2,1)} %get-tuple-element.32) | data formatting | bytes 524288
  109.0 6.8 %copy.29 = bf16[1,576,6144]{2,1,0:T(8,128)(2,1)} copy(bf16[1,576,6144]{2,1,0:T(8,128)(2,1)} %bitcast.4) | data formatting | bytes 14155776

commit v2 on v1

--- a/solution.py
+++ b/solution.py
@@ -89,10 +89,10 @@
 
 def kernel(
     q_hbm, k_hbm, v_hbm, g_hbm, moe_hbm, hid_hbm, w_hbm, decay, gates, ids,
-    qg_hbm, kg_hbm, vg_hbm, ho_hbm, wg_hbm, gate_out,
-    qb, kb, vb, gb, moe, hid, hid_t, w, x, pack, sel, back, acc, wg, ho, parts_c,
-    parts_s, parts_r, tok_s, tok_r, st_s, st_r, res_s, res_r, cum, qo, ko, vo,
-    load_sem, out_sem, z_send, z_recv, a_send, a_recv, b_send, b_recv,
+    qo, ko, vo, ho_out, wg, gate_out,
+    qb, kb, vb, gb, moe, hid, hid_t, order, w, x, pack, sel, back, acc, ho, parts,
+    parts_s, parts_r, tok_s, tok_r, st_s, st_r, res_s, res_r, cum,
+    load_sem, z_send, z_recv, a_send, a_recv, b_send, b_recv,
     x_send, x_recv, p_send, p_recv, t_send, t_recv,
 ):
     n_seq, n_exp = lax.axis_size("seq"), lax.axis_size("exp")
@@ -101,7 +101,7 @@
     cap = x.shape[0] // n_seq
     feat = moe.shape[1]
     width = w.shape[1]
-    heads = decay.shape[1]
+    heads = decay.shape[0]
     quarter = width // 4
 
     def seq_at(off):
@@ -113,16 +113,11 @@
             device_id=where, device_id_type=MESH,
         )
 
-    loads = [(moe_hbm, moe), (q_hbm, qb), (k_hbm, kb), (v_hbm, vb), (g_hbm, gb)]
+    loads = [
+        (moe_hbm, moe), (q_hbm, qb), (k_hbm, kb), (v_hbm, vb), (g_hbm, gb), (hid_hbm, hid), (w_hbm, w)
+    ]
     loads = [pltpu.make_async_copy(a, b, load_sem.at[i]) for i, (a, b) in enumerate(loads)]
-    n_load = len(loads)
-    hid_loads = []
-    for i, off in enumerate(OFFS):
-        start = pl.multiple_of(seq_at(off) * cap, 16)
-        hid_loads.append(pltpu.make_async_copy(
-            hid_hbm.at[pl.ds(start, cap)], hid.at[pl.ds(i * cap, cap)], load_sem.at[n_load + i]))
-    w_load = pltpu.make_async_copy(w_hbm, w, load_sem.at[n_load + n_seq])
-    for c in loads + hid_loads + [w_load]:
+    for c in loads:
         c.start()
 
     barrier = pltpu.get_barrier_semaphore()
@@ -134,7 +129,7 @@
     ids_f = ids[...].astype(F32)
     gates_f = gates[...].astype(F32)
     e_f = e.astype(F32)
-    id_rows = [to_row(ids_f[:, k:k + 1], 128) for k in range(2)]
+    id_rows = [ids_f[k:k + 1, :] for k in range(2)]
     expert = iota((n_exp, 128), 0).astype(F32)
     routed = jnp.where((expert == id_rows[0]) | (expert == id_rows[1]), 1.0, 0.0)
     upto = jnp.where(iota((128, 128), 0) <= iota((128, 128), 1), 1.0, 0.0).astype(BF)
@@ -148,8 +143,8 @@
     own_rank = jnp.max(jnp.where(expert == e_f, rank, -1.0), axis=0, keepdims=True)
     own = jnp.where(own_rank == slot_no, 1.0, 0.0)
     sel[...] = own
-    tok_gate = sum(jnp.where(ids_f[:, k:k + 1] == e_f, gates_f[:, k:k + 1], 0.0) for k in range(2))
-    slot_gate = jnp.sum(own * to_row(tok_gate, 128), axis=1, keepdims=True)
+    tok_gate = sum(jnp.where(id_rows[k] == e_f, gates_f[k:k + 1, :], 0.0) for k in range(2))
+    slot_gate = jnp.sum(own * tok_gate, axis=1, keepdims=True)
     x[0:cap, width:] = jnp.broadcast_to(slot_gate, (cap, 128)).astype(BF)
 
     pl.semaphore_wait(barrier, n_seq - 1 + n_exp - 1)
@@ -165,18 +160,18 @@
     x[0:cap, col_here] = pack[pl.ds(pl.multiple_of(e * cap, 16), cap), :]
 
     cum[...] = jnp.dot(
-        jnp.where(iota((128, 128), 0) >= iota((128, 128), 1), 1.0, 0.0), decay[...],
+        decay[...], jnp.where(iota((128, 128), 0) <= iota((128, 128), 1), 1.0, 0.0),
         preferred_element_type=F32, precision=lax.Precision.HIGHEST)
-    for c in loads[1:]:
+    for c in loads[1:5]:
         c.wait()
 
     def head_terms(h):
-        here = iota((128, heads), 1) == h
-        col = jnp.sum(jnp.where(here, cum[...], 0.0), axis=1, keepdims=True)
-        return col, col[127:128, :]
+        row = jnp.sum(jnp.where(iota((heads, 128), 0) == h, cum[...], 0.0), axis=0, keepdims=True)
+        col = to_col(row)
+        return row, col, col[127:128, :]
 
     def local_state(h, carry):
-        col, total = head_terms(h)
+        row, col, total = head_terms(h)
         cols = pl.ds(pl.multiple_of(h * 128, 128), 128)
         kw = (kb[:, cols].astype(F32) * jnp.exp(total - col)).T.astype(BF)
         qw = (qb[:, cols].astype(F32) * jnp.exp(col)).T.astype(BF)
@@ -186,8 +181,8 @@
         hi = gain.astype(BF).astype(F32)
         mid = (gain - hi).astype(BF).astype(F32)
         low = gain - hi - mid
-        row = iota((16, 128), 0)
-        three = jnp.where(row == 0, hi, jnp.where(row == 1, mid, jnp.where(row == 2, low, 0.0))).astype(BF)
+        line = iota((16, 128), 0)
+        three = jnp.where(line == 0, hi, jnp.where(line == 1, mid, jnp.where(line == 2, low, 0.0))).astype(BF)
         for p in range(2):
             st_s[2 * h + p, 0:64, :] = kv[64 * p:64 * p + 64, :]
             st_s[2 * h + p, 64:128, :] = qg[64 * p:64 * p + 64, :]
@@ -250,15 +245,22 @@
         b_copies[-1].start()
     res_r[me] = res_s[me]
 
-    for c in hid_loads:
-        c.wait()
-
-    def turn(i, carry):
-        rows = pl.ds(pl.multiple_of(i * 128, 128), 128)
-        hid_t[:, rows] = hid[rows, :].astype(F32).T.astype(BF)
+    n_rows = x.shape[0]
+    place = iota((1, n_rows), 1)
+    source = place
+    for i, off in enumerate(OFFS):
+        inside = (place >= i * cap) & (place < (i + 1) * cap)
+        source = source + jnp.where(inside, (seq_at(off) - i) * cap, 0)
+
+    def make_order(i, carry):
+        first = pl.multiple_of(i * 64, 64)
+        hit = iota((64, n_rows), 0) + first == source
+        order[pl.ds(first, 64), :] = jnp.where(hit, 1.0, 0.0).astype(BF)
         return carry
 
-    lax.fori_loop(0, hid.shape[0] // 128, turn, 0)
+    lax.fori_loop(0, n_rows // 64, make_order, 0)
+    loads[5].wait()
+    hid_t[...] = nn(hid[...], order[...]).astype(BF)
 
     go(ROUND1)
 
@@ -266,14 +268,14 @@
         c.wait_recv()
 
     def finish_head(h, carry):
-        col, total = head_terms(h)
+        row, col, total = head_terms(h)
         cols = pl.ds(pl.multiple_of(h * 128, 128), 128)
         q, k, v, g = qb[:, cols], kb[:, cols], vb[:, cols], gb[:, cols]
         two = res_r[pl.ds(2 * h, 2)]
         inc = two[:, 0:64, :].reshape(128, 128)
         upc = two[:, 64:128, :].reshape(128, 128)
         lead, tail = jnp.exp(col), jnp.exp(total - col)
-        spread = jnp.broadcast_to(col, (128, 128)) - to_row(col, 128)
+        spread = jnp.broadcast_to(col, (128, 128)) - jnp.broadcast_to(row, (128, 128))
         causal = iota((128, 128), 0) >= iota((128, 128), 1)
         mask = jnp.exp(jnp.where(causal, spread, -jnp.inf))
         gs = nt(g, v) * mask
@@ -284,62 +286,53 @@
         return carry
 
     lax.fori_loop(0, heads, finish_head, 0)
-    outs = [(qo, qg_hbm), (ko, kg_hbm), (vo, vg_hbm)]
-    outs = [pltpu.make_async_copy(a, b, out_sem.at[i]) for i, (a, b) in enumerate(outs)]
-    for c in outs:
-        c.start()
-
     go(ROUND2)
 
     chunk = 512
     chunks = width // chunk
-    n_rows = x.shape[0]
     cut = 512
+    units = w.shape[0]
 
     def product(start, count):
         rows = pl.ds(start, count)
-        back[rows, :] = jnp.zeros((count, back.shape[1]), F32)
+        back[:, rows] = jnp.zeros((units, count), F32)
 
         def one(i, carry):
             cols = pl.ds(pl.multiple_of(i * chunk, chunk), chunk)
-            back[rows, :] += nt(x[rows, cols], w[:, cols])
+            back[:, rows] += nt(w[:, cols], x[rows, cols])
             return carry
 
         lax.fori_loop(0, chunks, one, 0)
-
-        def after(i, carry):
-            part = pl.ds(pl.multiple_of(start + i * 64, 64), 64)
-            b = back[part, :]
-            gate = x[part, width:][:, 0:1].astype(F32)
-            ho[part, :] = (gate * b).astype(BF)
-            total = jnp.sum(b * hid[part, :].astype(F32), axis=1, keepdims=True)
-            parts_c[part, :] = jnp.broadcast_to(total, (64, 128))
-            return carry
-
-        lax.fori_loop(0, count // 64, after, 0)
+        first = jnp.where(iota((8, 128), 1) == 0, 1.0, 0.0).astype(BF)
+        gate = nt(first, x[rows, width:])[0:1, :]
+
+        def after(i, total):
+            part = pl.ds(pl.multiple_of(i * 64, 64), 64)
+            b = back[part, rows]
+            ho[part, rows] = (gate * b).astype(BF)
+            return total + jnp.sum(b * hid_t[part, rows].astype(F32), axis=0, keepdims=True)
+
+        total = lax.fori_loop(0, units // 64, after, jnp.zeros((1, count), F32))
+        parts[0:1, rows] = total
 
     def scaled(start, count, cols):
         rows = pl.ds(start, count)
         gate = x[rows, width:]
         return x[rows, cols] * jnp.concatenate([gate] * (chunk // 128), axis=1)
 
-    p_copies, ho_copies = [], []
+    p_copies = []
+    parts_s[...] = jnp.zeros_like(parts_s)
 
     def hand_out(first, last):
         for i in range(first, last):
-            rows = pl.ds(i * cap, cap)
-            parts_s[i] = jnp.broadcast_to(to_row(parts_c[rows, :][:, 0:1], cap), (8, 128))
-            owner = seq_at(OFFS[i])
-            c = pltpu.make_async_copy(
-                ho.at[rows], ho_hbm.at[pl.ds(pl.multiple_of(owner * cap, 16), cap)], out_sem.at[3 + i])
-            c.start()
-            ho_copies.append(c)
+            parts_s[i, 0:1, 0:cap] = parts[0:1, i * cap:(i + 1) * cap]
             if i > 0:
-                c = remote(parts_s.at[i], parts_r.at[i], p_send.at[i], p_recv.at[i], {"seq": owner})
+                owner = {"seq": seq_at(OFFS[i])}
+                c = remote(parts_s.at[i], parts_r.at[i], p_send.at[i], p_recv.at[i], owner)
                 c.start()
                 p_copies.append(c)
 
-    w_load.wait()
+    loads[6].wait()
     product(0, cut)
     go(ROUND3)
     hand_out(0, cut // cap)
@@ -354,17 +347,13 @@
     product(cut, n_rows - cut)
     hand_out(cut // cap, n_seq)
 
-    def wg_copy(i):
-        cols = pl.ds(pl.multiple_of(i * chunk, chunk), chunk)
-        return pltpu.make_async_copy(wg.at[:, cols], wg_hbm.at[:, cols], out_sem.at[3 + n_seq + i])
-
     def last_grad(i, carry):
         cols = pl.ds(pl.multiple_of(i * chunk, chunk), chunk)
         wg[:, cols] = (acc[:, cols] + nn(hid_t[:, cut:], scaled(cut, n_rows - cut, cols))).astype(BF)
-        wg_copy(i).start()
         return carry
 
     lax.fori_loop(0, chunks, last_grad, 0)
+    ho_out[...] = nt(ho[...], order[...]).astype(BF)
 
     total = parts_s[0]
     for i, c in enumerate(p_copies):
@@ -380,20 +369,23 @@
     tok_r[e] = tok_s[...]
     for c in t_copies:
         c.wait_recv()
-    by_expert = [to_col(tok_r[i, 0:1, :]) for i in range(n_exp)]
-    result = []
     for k in range(2):
-        result.append(sum(jnp.where(ids_f[:, k:k + 1] == float(i), by_expert[i], 0.0) for i in range(n_exp)))
-    gate_out[...] = jnp.where(iota((128, 2), 1) == 0, result[0], result[1])
+        gate_out[k:k + 1, :] = sum(
+            jnp.where(id_rows[k] == float(i), tok_r[i, 0:1, :], 0.0) for i in range(n_exp))
 
     for c in z_copies + a_copies + b_copies + p_copies + t_copies:
         c.wait_send()
     for m in MSGS:
         message(m).wait_send()
-    for c in outs + ho_copies:
+
+
+def write_out(*refs):
+    n = (len(refs) - 1) // 2
+    copies = [pltpu.make_async_copy(a, b, refs[-1].at[i]) for i, (a, b) in enumerate(zip(refs[:n], refs[n:-1]))]
+    for c in copies:
+        c.start()
+    for c in copies:
         c.wait()
-    for i in range(chunks):
-        wg_copy(i).wait()
 
 
 def on_device(
@@ -409,41 +401,46 @@
     dma = pltpu.SemaphoreType.DMA
     V = pltpu.VMEM
     wide = V((toks, flat), BF)
-    out = pl.pallas_call(
+    shapes = [
+        ((toks, flat), BF), ((toks, flat), BF), ((toks, flat), BF),
+        ((units, slots), BF), ((units, width), BF), ((2, toks), F32),
+    ]
+    held = pl.pallas_call(
         kernel,
-        out_shape=(
-            jax.ShapeDtypeStruct((toks, flat), BF),
-            jax.ShapeDtypeStruct((toks, flat), BF),
-            jax.ShapeDtypeStruct((toks, flat), BF),
-            jax.ShapeDtypeStruct((slots, units), BF),
-            jax.ShapeDtypeStruct((units, width), BF),
-            jax.ShapeDtypeStruct(gate_probs.shape, F32),
-        ),
+        out_shape=tuple(V(*s) for s in shapes),
         in_specs=[hbm] * 7 + [vmem] * 3,
-        out_specs=(hbm,) * 5 + (vmem,),
+        out_specs=(vmem,) * 6,
         scratch_shapes=[
             wide, wide, wide, wide, V((toks, feat), BF),
-            V((slots, units), BF), V((units, slots), BF), V((units, width), BF),
+            V((units, slots), BF), V((units, slots), BF), V((slots, slots), BF), V((units, width), BF),
             V((slots, width + 128), BF), V((n_exp * slots // n_seq, feat), BF),
-            V((slots // n_seq, 128), F32), V((slots, units), F32), V((units, width), F32),
-            V((units, width), BF), V((slots, units), BF), V((slots, 128), F32),
+            V((slots // n_seq, 128), F32), V((units, slots), F32), V((units, width), F32),
+            V((units, slots), BF), V((8, slots), F32),
             V((n_seq, 8, 128), F32), V((n_seq, 8, 128), F32),
             V((8, 128), F32), V((n_exp, 8, 128), F32),
             V((n_seq, 144, 128), BF), V((n_seq, 144, 128), BF),
             V((n_seq, 128, 128), BF), V((n_seq, 128, 128), BF),
-            V(log_decay.shape, F32), wide, wide, wide,
-            dma((5 + n_seq + 1,)), dma((3 + n_seq + width // 512,)),
+            V(log_decay.shape[::-1], F32),
+            dma((7,)),
             dma((n_exp,)), dma((n_exp,)), dma((n_seq,)), dma((n_seq,)), dma((n_seq,)), dma((n_seq,)),
             dma((len(MSGS),)), dma((len(MSGS),)), dma((n_seq,)), dma((n_seq,)), dma((n_exp,)), dma((n_exp,)),
         ],
         compiler_params=pltpu.CompilerParams(
-            collective_id=0, has_side_effects=True, vmem_limit_bytes=60 * 1024 * 1024
+            collective_id=0, has_side_effects=True, vmem_limit_bytes=48 * 1024 * 1024
         ),
     )(
-        queries, keys, values, attn_grad, moe_grad, hidden_acts[0], down_weight[0],
-        log_decay, gate_probs, expert_ids,
+        queries, keys, values, attn_grad, moe_grad, hidden_acts[0].T, down_weight[0],
+        log_decay.T, gate_probs.T, expert_ids.T,
     )
-    return (*out[:3], out[3][None], out[4][None], out[5])
+    out = pl.pallas_call(
+        write_out,
+        out_shape=tuple(jax.ShapeDtypeStruct(*s) for s in shapes),
+        in_specs=[vmem] * 6,
+        out_specs=(hbm,) * 6,
+        scratch_shapes=[dma((6,))],
+        compiler_params=pltpu.CompilerParams(vmem_limit_bytes=1024 * 1024),
+    )(*held)
+    return (*out[:3], out[3].T[None], out[4][None], out[5].T)
 
 
 def solution(mesh):

time: 116 us -> 95.3 us (0.82)
  local copies, waits for them, and re-layouts: 21.9 us -> 0 us
  Pallas kernels: 93.3 us -> 94.5 us
    unnamed x10 -> x0, local copies, waits for them, and re-layouts: 21.9 us -> none
    pallas_call x1 -> x2, Pallas kernels: 93.3 us -> 94.5 us  [the longest x1 90.9 us: on_device(): pl.pallas_call(kernel, out_shape=tuple((V(*s) for s in shapes)), in_specs...]
where the time goes in v2:
time: 95.3 us; the launch traced here: 95.1 us
  Pallas kernels  94.5 us (99%)
    pallas_call x1, Pallas kernels, on_device(): pl.pallas_call(kernel, out_shape=tuple((V(*s) for s in shapes)), in_specs...  90.9 us
    pallas_call x1, Pallas kernels, on_device(): pl.pallas_call(write_out, out_shape=tuple((jax.ShapeDtypeStruct(*s) for s...  3.57 us

profile of v2, /device:TPU:1, one launch (start us, length us, event | category | flops | bytes accessed | tf_op | source)
XLA Modules:
  0.0 95.1 jit_solution(5051041375383419276)
XLA Ops:
  0.6 90.9 %shard_map.145 = (bf16[128,1024]{1,0:T(8,128)(2,1)S(1)}, bf16[128,1024]{1,0:T(8,128)(2,1)S(1)}, bf16[128,1024]{1,0:T(8,128)(2,1)S(1)}, bf16[576,768]{1,0:T(8,128...) custom-call(bf16[128,1024]{1,0:T(8,128)(2,1)} %q_hbm.1, bf16[128,1024]{1,0:T(8,128)(2,1)} %k_hbm.1, ...), custom_call_target="tpu_custom_call" | custom-call | tf_op jit(solution)/shard_map/pallas_call | solution.py:408
  91.6 3.6 %shard_map.146 = (bf16[128,1024]{1,0:T(8,128)(2,1)}, bf16[128,1024]{1,0:T(8,128)(2,1)}, bf16[128,1024]{1,0:T(8,128)(2,1)}, bf16[576,768]{1,0:T(8,128)(2,1)}, bf1...) custom-call(bf16[128,1024]{1,0:T(8,128)(2,1)S(1)} %get-tuple-element.18.refs_0_, ...), custom_call_target="tpu_custom_call" | custom-call | tf_op jit(solution)/shard_map/pallas_call | solution.py:435

commit v3 on v2

--- a/solution.py
+++ b/solution.py
@@ -19,19 +19,36 @@
 DIRS = {"xp": (1, 0), "xm": (-1, 0), "yp": (0, 1), "ym": (0, -1)}
 H1, H2, H1b, H1a, H2a, H2b = (0, 2), (2, 4), (0, 1), (1, 2), (2, 3), (3, 4)
 
-START = [
-    ("xp", (0, 0), H1), ("xm", (0, 0), H1), ("yp", (0, 0), H2), ("ym", (0, 0), H2),
-    ("xp", (0, 0), H2), ("xm", (0, 0), H2), ("yp", (0, 0), H1), ("ym", (0, 0), H1),
-]
+NZ = 4
+REL = [(0, 0), (0, 1), (1, 0), (1, 1), (-1, 0), (-1, 1), (2, 0), (2, 1)]
+REL_SLOT = {r: i for i, r in enumerate(REL)}
+
+START = [[(d, (0, 0), q) for d in ("xp", "xm", "yp", "ym")] for q in (H1b, H1a, H2a, H2b)]
 ROUND1 = [
-    ([("xp", (0, 0), H1)], [("xp", (-1, 0), H1a), ("yp", (-1, 0), H1), ("ym", (-1, 0), H1)]),
-    ([("xm", (0, 0), H1)], [("xm", (1, 0), H1b), ("yp", (1, 0), H1), ("ym", (1, 0), H1)]),
-    ([("yp", (0, 0), H2)], [("yp", (0, -1), H2a), ("xp", (0, -1), H2), ("xm", (0, -1), H2)]),
-    ([("ym", (0, 0), H2)], [("ym", (0, 1), H2b), ("xp", (0, 1), H2), ("xm", (0, 1), H2)]),
-    ([("xp", (0, 0), H2)], [("xp", (-1, 0), H2a)]),
-    ([("xm", (0, 0), H2)], [("xm", (1, 0), H2b)]),
-    ([("yp", (0, 0), H1)], [("yp", (0, -1), H1a)]),
-    ([("ym", (0, 0), H1)], [("ym", (0, 1), H1b)]),
+    [
+        ([("xp", (0, 0), H1b)], []),
+        ([("xm", (0, 0), H1b)], [("xm", (1, 0), H1b)]),
+        ([("ym", (0, 0), H1b)], [("ym", (0, 1), H1b)]),
+        ([("yp", (0, 0), H1b)], []),
+    ],
+    [
+        ([("xp", (0, 0), H1a)], [("xp", (-1, 0), H1a), ("yp", (-1, 0), H1), ("ym", (-1, 0), H1)]),
+        ([("xm", (0, 0), H1a)], [("yp", (1, 0), H1), ("ym", (1, 0), H1)]),
+        ([("yp", (0, 0), H1a)], [("yp", (0, -1), H1a)]),
+        ([("ym", (0, 0), H1a)], []),
+    ],
+    [
+        ([("yp", (0, 0), H2a)], [("yp", (0, -1), H2a)]),
+        ([("xp", (0, 0), H2a)], [("xp", (-1, 0), H2a)]),
+        ([("ym", (0, 0), H2a)], []),
+        ([("xm", (0, 0), H2a)], []),
+    ],
+    [
+        ([("yp", (0, 0), H2b)], [("xp", (0, -1), H2), ("xm", (0, -1), H2)]),
+        ([("ym", (0, 0), H2b)], [("ym", (0, 1), H2b), ("xp", (0, 1), H2), ("xm", (0, 1), H2)]),
+        ([("xm", (0, 0), H2b)], [("xm", (1, 0), H2b)]),
+        ([("xp", (0, 0), H2b)], []),
+    ],
 ]
 ROUND2 = [
     ([("xp", (-1, 0), H1a), ("xm", (1, 0), H1b)], [("yp", (2, 0), H1), ("ym", (2, 0), H1)]),
@@ -57,8 +74,28 @@
     ([("yp", (-1, -1), H1a), ("yp", (1, -1), H1a), ("ym", (-1, 1), H1b), ("ym", (1, 1), H1b)], []),
     ([("yp", (2, -1), H1a), ("ym", (2, 1), H1b), ("xp", (-1, 2), H2a), ("xm", (1, 2), H2b)], []),
 ]
-MSGS = START + [m for r in (ROUND1, ROUND2, ROUND3) for _, sends in r for m in sends]
+MSGS = sum(START, []) + [m for r in (*ROUND1, ROUND2, ROUND3) for _, sends in r for m in sends]
 INDEX = {m: i for i, m in enumerate(MSGS)}
+
+FULL, A = (0, 4), (1, 3)
+RAW_START = [(d, (0, 0), FULL) for d in ("xp", "xm", "yp", "ym")]
+RAW1 = [
+    ([("xp", (0, 0), FULL)], [("xp", (-1, 0), A), ("yp", (-1, 0), H1), ("ym", (-1, 0), H1)]),
+    ([("xm", (0, 0), FULL)], [
+        ("xm", (1, 0), H1b), ("xm", (1, 0), H2b), ("yp", (1, 0), H1), ("ym", (1, 0), H1)]),
+    ([("yp", (0, 0), FULL)], [("yp", (0, -1), A), ("xp", (0, -1), H2), ("xm", (0, -1), H2)]),
+    ([("ym", (0, 0), FULL)], [
+        ("ym", (0, 1), H2b), ("ym", (0, 1), H1b), ("xp", (0, 1), H2), ("xm", (0, 1), H2)]),
+]
+RAW2 = [
+    ([("xp", (-1, 0), A), ("xm", (1, 0), H1b)], ROUND2[0][1]),
+    ([("yp", (0, -1), A), ("ym", (0, 1), H2b)], ROUND2[1][1]),
+    *ROUND2[2:10],
+    ([("xm", (1, 0), H2b), ("ym", (0, 1), H1b)], []),
+]
+RAW_MSGS = RAW_START + [m for r in (RAW1, RAW2, ROUND3) for _, sends in r for m in sends]
+RAW_INDEX = {m: i for i, m in enumerate(RAW_MSGS)}
+RAW = 256
 
 
 def wrap(a, d):
@@ -90,10 +127,10 @@
 def kernel(
     q_hbm, k_hbm, v_hbm, g_hbm, moe_hbm, hid_hbm, w_hbm, decay, gates, ids,
     qo, ko, vo, ho_out, wg, gate_out,
-    qb, kb, vb, gb, moe, hid, hid_t, order, w, x, pack, sel, back, acc, ho, parts,
+    qb, kb, vb, gb, moe, raw, raw_pack, hid, hid_t, order, w, x, pack, sel, back, acc, ho, parts,
     parts_s, parts_r, tok_s, tok_r, st_s, st_r, res_s, res_r, cum,
     load_sem, z_send, z_recv, a_send, a_recv, b_send, b_recv,
-    x_send, x_recv, p_send, p_recv, t_send, t_recv,
+    x_send, x_recv, r_send, r_recv, y_send, y_recv, p_send, p_recv, t_send, t_recv,
 ):
     n_seq, n_exp = lax.axis_size("seq"), lax.axis_size("exp")
     me, e = lax.axis_index("seq"), lax.axis_index("exp")
@@ -102,7 +139,16 @@
     feat = moe.shape[1]
     width = w.shape[1]
     heads = decay.shape[0]
-    quarter = width // 4
+    toks = moe.shape[0]
+    tall = toks + 16
+    thin = feat - RAW
+    gate_at = n_exp * thin
+    raw_at = gate_at + 128
+    quarter = gate_at // 4
+    my_z, my_core = e // 2, e % 2
+
+    def exp_at(rel):
+        return ((my_z + rel[0] + NZ) % NZ) * 2 + (my_core + rel[1]) % 2
 
     def seq_at(off):
         return ((my_y + off[1] + NY) % NY) * NX + (my_x + off[0] + NX) % NX
@@ -114,8 +160,13 @@
         )
 
     loads = [
-        (moe_hbm, moe), (q_hbm, qb), (k_hbm, kb), (v_hbm, vb), (g_hbm, gb), (hid_hbm, hid), (w_hbm, w)
+        (moe_hbm, moe), (q_hbm, qb), (k_hbm, kb), (v_hbm, vb), (g_hbm, gb), (hid_hbm, hid)
     ]
+    loads.append((moe_hbm.at[:, pl.ds(thin, RAW)], raw.at[pl.ds(0, toks)]))
+    for i, rel in enumerate(REL):
+        first = pl.multiple_of(exp_at(rel) * feat, 128)
+        loads.append((w_hbm.at[:, pl.ds(first, thin)], w.at[:, pl.ds(i * thin, thin)]))
+        loads.append((w_hbm.at[:, pl.ds(first + thin, RAW)], w.at[:, pl.ds(gate_at + i * RAW, RAW)]))
     loads = [pltpu.make_async_copy(a, b, load_sem.at[i]) for i, (a, b) in enumerate(loads)]
     for c in loads:
         c.start()
@@ -126,10 +177,51 @@
     for off in range(1, n_exp):
         pl.semaphore_signal(barrier, inc=1, device_id={"exp": (e + off) % n_exp}, device_id_type=MESH)
 
+    def span(q):
+        stop = raw_at if q[1] == 4 else q[1] * quarter
+        return pl.ds(q[0] * quarter, stop - q[0] * quarter)
+
+    def message(m):
+        d, off, q = m
+        i = INDEX[m]
+        src = x.at[pl.ds(SLOT[off] * cap, cap), span(q)]
+        dst = x.at[pl.ds(SLOT[wrap(off, DIRS[d])] * cap, cap), span(q)]
+        return remote(src, dst, x_send.at[i], x_recv.at[i], {"seq": seq_at(DIRS[d])})
+
+    def go(steps):
+        for waits, sends in steps:
+            for m in waits:
+                message(m).wait_recv()
+            for m in sends:
+                message(m).start()
+
+    def raw_message(m):
+        d, off, q = m
+        i = RAW_INDEX[m]
+        first = q[0] * toks // 4
+        count = (tall if q[1] == 4 else q[1] * toks // 4) - first
+        src = raw.at[pl.ds(SLOT[off] * tall + first, count)]
+        dst = raw.at[pl.ds(SLOT[wrap(off, DIRS[d])] * tall + first, count)]
+        return remote(src, dst, r_send.at[i], r_recv.at[i], {"seq": seq_at(DIRS[d])})
+
+    def go_raw(steps):
+        for waits, sends in steps:
+            for m in waits:
+                raw_message(m).wait_recv()
+            for m in sends:
+                raw_message(m).start()
+
     ids_f = ids[...].astype(F32)
     gates_f = gates[...].astype(F32)
     e_f = e.astype(F32)
     id_rows = [ids_f[k:k + 1, :] for k in range(2)]
+    line = iota((16, 128), 0)
+    id_tile = jnp.where(line == 0, id_rows[0], jnp.where(line == 1, id_rows[1], 0.0)).astype(BF)
+    raw[toks:tall, :] = jnp.concatenate([id_tile] * (RAW // 128), axis=1)
+    loads[6].wait()
+    pl.semaphore_wait(barrier, n_seq - 1 + n_exp - 1)
+    go_raw([([], RAW_START)])
+
     expert = iota((n_exp, 128), 0).astype(F32)
     routed = jnp.where((expert == id_rows[0]) | (expert == id_rows[1]), 1.0, 0.0)
     upto = jnp.where(iota((128, 128), 0) <= iota((128, 128), 1), 1.0, 0.0).astype(BF)
@@ -139,25 +231,36 @@
     loads[0].wait()
     for i in range(n_exp):
         chosen = jnp.where(rank[i:i + 1, :] == slot_no, 1.0, 0.0)
-        pack[pl.ds(i * cap, cap), :] = nn(chosen.astype(BF), moe[...]).astype(BF)
+        pack[pl.ds(i * cap, cap), :] = nn(chosen.astype(BF), moe[:, 0:thin]).astype(BF)
     own_rank = jnp.max(jnp.where(expert == e_f, rank, -1.0), axis=0, keepdims=True)
     own = jnp.where(own_rank == slot_no, 1.0, 0.0)
     sel[...] = own
     tok_gate = sum(jnp.where(id_rows[k] == e_f, gates_f[k:k + 1, :], 0.0) for k in range(2))
     slot_gate = jnp.sum(own * tok_gate, axis=1, keepdims=True)
-    x[0:cap, width:] = jnp.broadcast_to(slot_gate, (cap, 128)).astype(BF)
-
-    pl.semaphore_wait(barrier, n_seq - 1 + n_exp - 1)
-
-    col_here = pl.ds(pl.multiple_of(e * feat, 128), feat)
+    x[0:cap, gate_at:raw_at] = jnp.broadcast_to(slot_gate, (cap, 128)).astype(BF)
+
     z_copies = []
-    for off in range(1, n_exp):
-        peer = (e + off) % n_exp
-        z_copies.append(remote(
-            pack.at[pl.ds(pl.multiple_of(peer * cap, 16), cap)], x.at[pl.ds(0, cap), col_here],
-            z_send.at[off], z_recv.at[off], {"exp": peer}))
-        z_copies[-1].start()
-    x[0:cap, col_here] = pack[pl.ds(pl.multiple_of(e * cap, 16), cap), :]
+    for i, rel in enumerate(REL):
+        if i > 0:
+            peer = exp_at(rel)
+            there = REL_SLOT[((-rel[0] + 1) % NZ - 1, rel[1])]
+            z_copies.append(remote(
+                pack.at[pl.ds(pl.multiple_of(peer * cap, 16), cap)],
+                x.at[pl.ds(0, cap), pl.ds(there * thin, thin)],
+                z_send.at[there], z_recv.at[there], {"exp": peer}))
+            z_copies[-1].start()
+    z_recvs = [
+        remote(pack.at[pl.ds(0, cap)], x.at[pl.ds(0, cap), pl.ds(i * thin, thin)],
+               z_send.at[i], z_recv.at[i], {"exp": exp_at(REL[i])}) for i in range(1, n_exp)]
+    x[0:cap, 0:thin] = pack[pl.ds(pl.multiple_of(e * cap, 16), cap), :]
+
+    def begin(i):
+        for c in z_recvs[max(2 * i - 1, 0):2 * i + 1]:
+            c.wait_recv()
+        go([([], START[i])])
+
+    go_raw(RAW1)
+    begin(0)
 
     cum[...] = jnp.dot(
         decay[...], jnp.where(iota((128, 128), 0) <= iota((128, 128), 1), 1.0, 0.0),
@@ -181,7 +284,6 @@
         hi = gain.astype(BF).astype(F32)
         mid = (gain - hi).astype(BF).astype(F32)
         low = gain - hi - mid
-        line = iota((16, 128), 0)
         three = jnp.where(line == 0, hi, jnp.where(line == 1, mid, jnp.where(line == 2, low, 0.0))).astype(BF)
         for p in range(2):
             st_s[2 * h + p, 0:64, :] = kv[64 * p:64 * p + 64, :]
@@ -190,34 +292,69 @@
         return carry
 
     lax.fori_loop(0, heads, local_state, 0)
+    go_raw(RAW2)
+    begin(1)
+    go_raw(ROUND3)
     a_copies = []
     for off in range(1, n_seq):
         peer = (me + off) % n_seq
         a_copies.append(remote(st_s.at[peer], st_r.at[me], a_send.at[off], a_recv.at[off], {"seq": peer}))
         a_copies[-1].start()
     st_r[me] = st_s[me]
-
-    def span(q):
-        stop = width + 128 if q[1] == 4 else q[1] * quarter
-        return pl.ds(q[0] * quarter, stop - q[0] * quarter)
-
-    def message(m):
-        d, off, q = m
-        i = INDEX[m]
-        src = x.at[pl.ds(SLOT[off] * cap, cap), span(q)]
-        dst = x.at[pl.ds(SLOT[wrap(off, DIRS[d])] * cap, cap), span(q)]
-        return remote(src, dst, x_send.at[i], x_recv.at[i], {"seq": seq_at(DIRS[d])})
-
-    def go(steps):
-        for waits, sends in steps:
-            for m in waits:
-                message(m).wait_recv()
-            for m in sends:
-                message(m).start()
-
-    for c in z_copies:
-        c.wait_recv()
-    go([([], START)])
+    begin(2)
+    begin(3)
+
+    n_rows = x.shape[0]
+    place = iota((1, n_rows), 1)
+    source = place
+    for i, off in enumerate(OFFS):
+        inside = (place >= i * cap) & (place < (i + 1) * cap)
+        source = source + jnp.where(inside, (seq_at(off) - i) * cap, 0)
+
+    def make_order(i, carry):
+        first = pl.multiple_of(i * 64, 64)
+        hit = iota((64, n_rows), 0) + first == source
+        order[pl.ds(first, 64), :] = jnp.where(hit, 1.0, 0.0).astype(BF)
+        return carry
+
+    lax.fori_loop(0, n_rows // 64, make_order, 0)
+    loads[5].wait()
+    hid_t[...] = nn(hid[...], order[...]).astype(BF)
+
+    go_raw(ROUND4)
+
+    def pack_block(i, carry):
+        tile = raw[pl.ds(pl.multiple_of(i * tall + toks, 16), 16), 0:128].astype(F32)
+        id0, id1 = tile[0:1, :], tile[1:2, :]
+        routed = jnp.where((expert == id0) | (expert == id1), 1.0, 0.0)
+        rank = jnp.where(routed > 0.0, nn(routed.astype(BF), upto) - 1.0, -1.0)
+        chosen = jnp.concatenate(
+            [jnp.where(rank[j:j + 1, :] == slot_no, 1.0, 0.0).astype(BF) for j in range(n_exp)], axis=0)
+        rows = nn(chosen, raw[pl.ds(pl.multiple_of(i * tall, 16), toks), :]).astype(BF)
+        for j in range(n_exp):
+            raw_pack[j, pl.ds(pl.multiple_of(i * cap, 16), cap), :] = rows[j * cap:(j + 1) * cap, :]
+        return carry
+
+    lax.fori_loop(0, n_seq, pack_block, 0)
+    cut = 512
+    y_copies, y_recvs = [], []
+    for part, (first, count) in enumerate([(0, cut), (cut, n_rows - cut)]):
+        rows = pl.ds(first, count)
+        y_recvs.append([])
+        for i, rel in enumerate(REL[1:], 1):
+            peer = exp_at(rel)
+            there = REL_SLOT[((-rel[0] + 1) % NZ - 1, rel[1])]
+            c = remote(
+                raw_pack.at[peer, rows], x.at[rows, pl.ds(raw_at + there * RAW, RAW)],
+                y_send.at[part, there], y_recv.at[part, there], {"exp": peer})
+            c.start()
+            y_copies.append(c)
+            y_recvs[-1].append(remote(
+                raw_pack.at[peer, rows], x.at[rows, pl.ds(raw_at + i * RAW, RAW)],
+                y_send.at[part, i], y_recv.at[part, i], {"exp": peer}))
+    x[:, raw_at:raw_at + RAW] = raw_pack[e]
+
+    go(ROUND1[0])
 
     for c in a_copies:
         c.wait_recv()
@@ -245,24 +382,8 @@
         b_copies[-1].start()
     res_r[me] = res_s[me]
 
-    n_rows = x.shape[0]
-    place = iota((1, n_rows), 1)
-    source = place
-    for i, off in enumerate(OFFS):
-        inside = (place >= i * cap) & (place < (i + 1) * cap)
-        source = source + jnp.where(inside, (seq_at(off) - i) * cap, 0)
-
-    def make_order(i, carry):
-        first = pl.multiple_of(i * 64, 64)
-        hit = iota((64, n_rows), 0) + first == source
-        order[pl.ds(first, 64), :] = jnp.where(hit, 1.0, 0.0).astype(BF)
-        return carry
-
-    lax.fori_loop(0, n_rows // 64, make_order, 0)
-    loads[5].wait()
-    hid_t[...] = nn(hid[...], order[...]).astype(BF)
-
-    go(ROUND1)
+    for step in ROUND1[1:]:
+        go(step)
 
     for c in b_copies:
         c.wait_recv()
@@ -286,25 +407,32 @@
         return carry
 
     lax.fori_loop(0, heads, finish_head, 0)
-    go(ROUND2)
 
     chunk = 512
     chunks = width // chunk
-    cut = 512
     units = w.shape[0]
 
-    def product(start, count):
+    def x_cols(i):
+        return pl.ds(pl.multiple_of(i * chunk + jnp.where(i * chunk >= gate_at, 128, 0), 128), chunk)
+
+    wide = gate_at // chunk
+
+    def product(start, count, lo, hi):
         rows = pl.ds(start, count)
-        back[:, rows] = jnp.zeros((units, count), F32)
+        if lo == 0:
+            back[:, rows] = jnp.zeros((units, count), F32)
 
         def one(i, carry):
             cols = pl.ds(pl.multiple_of(i * chunk, chunk), chunk)
-            back[:, rows] += nt(w[:, cols], x[rows, cols])
+            back[:, rows] += nt(w[:, cols], x[rows, x_cols(i)])
             return carry
 
-        lax.fori_loop(0, chunks, one, 0)
+        lax.fori_loop(lo, hi, one, 0)
+
+    def use_product(start, count):
+        rows = pl.ds(start, count)
         first = jnp.where(iota((8, 128), 1) == 0, 1.0, 0.0).astype(BF)
-        gate = nt(first, x[rows, width:])[0:1, :]
+        gate = nt(first, x[rows, gate_at:raw_at])[0:1, :]
 
         def after(i, total):
             part = pl.ds(pl.multiple_of(i * 64, 64), 64)
@@ -317,7 +445,7 @@
 
     def scaled(start, count, cols):
         rows = pl.ds(start, count)
-        gate = x[rows, width:]
+        gate = x[rows, gate_at:raw_at]
         return x[rows, cols] * jnp.concatenate([gate] * (chunk // 128), axis=1)
 
     p_copies = []
@@ -332,24 +460,35 @@
                 c.start()
                 p_copies.append(c)
 
-    loads[6].wait()
-    product(0, cut)
-    go(ROUND3)
-    hand_out(0, cut // cap)
-
     def first_grad(i, carry):
         cols = pl.ds(pl.multiple_of(i * chunk, chunk), chunk)
-        acc[:, cols] = nn(hid_t[:, 0:cut], scaled(0, cut, cols))
+        acc[:, cols] = nn(hid_t[:, 0:cut], scaled(0, cut, x_cols(i)))
         return carry
 
-    lax.fori_loop(0, chunks, first_grad, 0)
+    for c in loads[7:]:
+        c.wait()
+    go(ROUND2[:6] + ROUND2[-1:])
+    product(0, cut // 2, 0, wide)
+    go(ROUND2[6:10])
+    product(cut // 2, cut // 2, 0, wide)
+    go(ROUND3)
+    lax.fori_loop(0, wide, first_grad, 0)
+    for c in y_recvs[0]:
+        c.wait_recv()
+    product(0, cut, wide, chunks)
+    use_product(0, cut)
+    hand_out(0, cut // cap)
+    lax.fori_loop(wide, chunks, first_grad, 0)
     go(ROUND4)
-    product(cut, n_rows - cut)
+    for c in y_recvs[1]:
+        c.wait_recv()
+    product(cut, n_rows - cut, 0, chunks)
+    use_product(cut, n_rows - cut)
     hand_out(cut // cap, n_seq)
 
     def last_grad(i, carry):
         cols = pl.ds(pl.multiple_of(i * chunk, chunk), chunk)
-        wg[:, cols] = (acc[:, cols] + nn(hid_t[:, cut:], scaled(cut, n_rows - cut, cols))).astype(BF)
+        wg[:, cols] = (acc[:, cols] + nn(hid_t[:, cut:], scaled(cut, n_rows - cut, x_cols(i)))).astype(BF)
         return carry
 
     lax.fori_loop(0, chunks, last_grad, 0)
@@ -373,15 +512,27 @@
         gate_out[k:k + 1, :] = sum(
             jnp.where(id_rows[k] == float(i), tok_r[i, 0:1, :], 0.0) for i in range(n_exp))
 
-    for c in z_copies + a_copies + b_copies + p_copies + t_copies:
+    for c in z_copies + y_copies + a_copies + b_copies + p_copies + t_copies:
         c.wait_send()
     for m in MSGS:
         message(m).wait_send()
-
-
-def write_out(*refs):
-    n = (len(refs) - 1) // 2
-    copies = [pltpu.make_async_copy(a, b, refs[-1].at[i]) for i, (a, b) in enumerate(zip(refs[:n], refs[n:-1]))]
+    for m in RAW_MSGS:
+        raw_message(m).wait_send()
+
+
+def write_out(q_in, k_in, v_in, ho_in, wg_in, gate_in, q_out, k_out, v_out, ho_out, wg_out, gate_out, sem):
+    e = lax.axis_index("exp")
+    feat = wg_in.shape[1] // len(REL)
+    thin = feat - RAW
+    pairs = []
+    for i, (z, core) in enumerate(REL):
+        there = ((e // 2 + z + NZ) % NZ) * 2 + (e % 2 + core) % 2
+        first = pl.multiple_of(there * feat, 128)
+        pairs.append((wg_in.at[:, pl.ds(i * thin, thin)], wg_out.at[:, pl.ds(first, thin)]))
+        raw_in = wg_in.at[:, pl.ds(len(REL) * thin + i * RAW, RAW)]
+        pairs.append((raw_in, wg_out.at[:, pl.ds(first + thin, RAW)]))
+    pairs += [(q_in, q_out), (k_in, k_out), (v_in, v_out), (ho_in, ho_out), (gate_in, gate_out)]
+    copies = [pltpu.make_async_copy(a, b, sem.at[i]) for i, (a, b) in enumerate(pairs)]
     for c in copies:
         c.start()
     for c in copies:
@@ -412,8 +563,8 @@
         out_specs=(vmem,) * 6,
         scratch_shapes=[
             wide, wide, wide, wide, V((toks, feat), BF),
-            V((units, slots), BF), V((units, slots), BF), V((slots, slots), BF), V((units, width), BF),
-            V((slots, width + 128), BF), V((n_exp * slots // n_seq, feat), BF),
+            V((n_seq * (toks + 16), RAW), BF), V((n_exp, slots, RAW), BF), V((units, slots), BF), V((units, slots), BF), V((slots, slots), BF), V((units, width), BF),
+            V((slots, width + 128), BF), V((n_exp * slots // n_seq, feat - RAW), BF),
             V((slots // n_seq, 128), F32), V((units, slots), F32), V((units, width), F32),
             V((units, slots), BF), V((8, slots), F32),
             V((n_seq, 8, 128), F32), V((n_seq, 8, 128), F32),
@@ -421,12 +572,13 @@
             V((n_seq, 144, 128), BF), V((n_seq, 144, 128), BF),
             V((n_seq, 128, 128), BF), V((n_seq, 128, 128), BF),
             V(log_decay.shape[::-1], F32),
-            dma((7,)),
+            dma((7 + 2 * n_exp,)),
             dma((n_exp,)), dma((n_exp,)), dma((n_seq,)), dma((n_seq,)), dma((n_seq,)), dma((n_seq,)),
-            dma((len(MSGS),)), dma((len(MSGS),)), dma((n_seq,)), dma((n_seq,)), dma((n_exp,)), dma((n_exp,)),
+            dma((len(MSGS),)), dma((len(MSGS),)), dma((len(RAW_MSGS),)), dma((len(RAW_MSGS),)),
+            dma((2, n_exp)), dma((2, n_exp)), dma((n_seq,)), dma((n_seq,)), dma((n_exp,)), dma((n_exp,)),
         ],
         compiler_params=pltpu.CompilerParams(
-            collective_id=0, has_side_effects=True, vmem_limit_bytes=48 * 1024 * 1024
+            collective_id=0, has_side_effects=True, vmem_limit_bytes=53 * 1024 * 1024
         ),
     )(
         queries, keys, values, attn_grad, moe_grad, hidden_acts[0].T, down_weight[0],
@@ -437,7 +589,7 @@
         out_shape=tuple(jax.ShapeDtypeStruct(*s) for s in shapes),
         in_specs=[vmem] * 6,
         out_specs=(hbm,) * 6,
-        scratch_shapes=[dma((6,))],
+        scratch_shapes=[dma((5 + 2 * n_exp,))],
         compiler_params=pltpu.CompilerParams(vmem_limit_bytes=1024 * 1024),
     )(*held)
     return (*out[:3], out[3].T[None], out[4][None], out[5].T)

time: 95.3 us -> 90.6 us (0.951)
  Pallas kernels: 94.5 us -> 89.8 us
    pallas_call x1, Pallas kernels: 90.9 us -> 86.2 us  [on_device(): pl.pallas_call(kernel, out_shape=tuple((V(*s) for s in shapes)), in_specs...]
where the time goes in v3:
time: 90.6 us; the launch traced here: 90.5 us
  Pallas kernels  89.8 us (99%)
    pallas_call x1, Pallas kernels, on_device(): pl.pallas_call(kernel, out_shape=tuple((V(*s) for s in shapes)), in_specs...  86.2 us
    pallas_call x1, Pallas kernels, on_device(): pl.pallas_call(write_out, out_shape=tuple((jax.ShapeDtypeStruct(*s) for s...  3.61 us

profile of v3, /device:TPU:1, one launch (start us, length us, event | category | flops | bytes accessed | tf_op | source)
XLA Modules:
  0.0 90.5 jit_solution(111005132813883416)
XLA Ops:
  0.6 86.2 %shard_map.145 = (bf16[128,1024]{1,0:T(8,128)(2,1)S(1)}, bf16[128,1024]{1,0:T(8,128)(2,1)S(1)}, bf16[128,1024]{1,0:T(8,128)(2,1)S(1)}, bf16[576,768]{1,0:T(8,128...) custom-call(bf16[128,1024]{1,0:T(8,128)(2,1)} %q_hbm.1, bf16[128,1024]{1,0:T(8,128)(2,1)} %k_hbm.1, ...), custom_call_target="tpu_custom_call" | custom-call | tf_op jit(solution)/shard_map/pallas_call | solution.py:559
  86.8 3.6 %shard_map.146 = (bf16[128,1024]{1,0:T(8,128)(2,1)}, bf16[128,1024]{1,0:T(8,128)(2,1)}, bf16[128,1024]{1,0:T(8,128)(2,1)}, bf16[576,768]{1,0:T(8,128)(2,1)}, bf1...) custom-call(bf16[128,1024]{1,0:T(8,128)(2,1)S(1)} %get-tuple-element.18.q_in, bf16[128,1024]{1,0:T(8,128)(2,1)S(1)} %get-tuple-element.19.k_in, ...), custom_call_target="tpu_custom_call" | custom-call | tf_op jit(solution)/shard_map/pallas_call | solution.py:587

commit v4 on v3

--- a/solution.py
+++ b/solution.py
@@ -168,7 +168,7 @@
         loads.append((w_hbm.at[:, pl.ds(first, thin)], w.at[:, pl.ds(i * thin, thin)]))
         loads.append((w_hbm.at[:, pl.ds(first + thin, RAW)], w.at[:, pl.ds(gate_at + i * RAW, RAW)]))
     loads = [pltpu.make_async_copy(a, b, load_sem.at[i]) for i, (a, b) in enumerate(loads)]
-    for c in loads:
+    for c in [loads[6]] + loads[:6]:
         c.start()
 
     barrier = pltpu.get_barrier_semaphore()
@@ -249,6 +249,8 @@
                 x.at[pl.ds(0, cap), pl.ds(there * thin, thin)],
                 z_send.at[there], z_recv.at[there], {"exp": peer}))
             z_copies[-1].start()
+    for c in loads[7:]:
+        c.start()
     z_recvs = [
         remote(pack.at[pl.ds(0, cap)], x.at[pl.ds(0, cap), pl.ds(i * thin, thin)],
                z_send.at[i], z_recv.at[i], {"exp": exp_at(REL[i])}) for i in range(1, n_exp)]
@@ -408,7 +410,7 @@
 
     lax.fori_loop(0, heads, finish_head, 0)
 
-    chunk = 512
+    chunk = 1024
     chunks = width // chunk
     units = w.shape[0]
 
@@ -480,9 +482,10 @@
     hand_out(0, cut // cap)
     lax.fori_loop(wide, chunks, first_grad, 0)
     go(ROUND4)
+    product(cut, n_rows - cut, 0, wide)
     for c in y_recvs[1]:
         c.wait_recv()
-    product(cut, n_rows - cut, 0, chunks)
+    product(cut, n_rows - cut, wide, chunks)
     use_product(cut, n_rows - cut)
     hand_out(cut // cap, n_seq)
 

time: 90.6 us -> 88.1 us (0.972)
  Pallas kernels: 89.8 us -> 87.3 us
    pallas_call x1, Pallas kernels: 86.2 us -> 83.7 us  [on_device(): pl.pallas_call(kernel, out_shape=tuple((V(*s) for s in shapes)), in_specs...]
where the time goes in v4:
time: 88.1 us; the launch traced here: 87.9 us
  Pallas kernels  87.3 us (99%)
    pallas_call x1, Pallas kernels, on_device(): pl.pallas_call(kernel, out_shape=tuple((V(*s) for s in shapes)), in_specs...  83.7 us
    pallas_call x1, Pallas kernels, on_device(): pl.pallas_call(write_out, out_shape=tuple((jax.ShapeDtypeStruct(*s) for s...  3.61 us

profile of v4, /device:TPU:1, one launch (start us, length us, event | category | flops | bytes accessed | tf_op | source)
XLA Modules:
  0.0 87.9 jit_solution(9931099367264999545)
XLA Ops:
  0.6 83.7 %shard_map.145 = (bf16[128,1024]{1,0:T(8,128)(2,1)S(1)}, bf16[128,1024]{1,0:T(8,128)(2,1)S(1)}, bf16[128,1024]{1,0:T(8,128)(2,1)S(1)}, bf16[576,768]{1,0:T(8,128...) custom-call(bf16[128,1024]{1,0:T(8,128)(2,1)} %q_hbm.1, bf16[128,1024]{1,0:T(8,128)(2,1)} %k_hbm.1, ...), custom_call_target="tpu_custom_call" | custom-call | tf_op jit(solution)/shard_map/pallas_call | solution.py:562
  84.3 3.6 %shard_map.146 = (bf16[128,1024]{1,0:T(8,128)(2,1)}, bf16[128,1024]{1,0:T(8,128)(2,1)}, bf16[128,1024]{1,0:T(8,128)(2,1)}, bf16[576,768]{1,0:T(8,128)(2,1)}, bf1...) custom-call(bf16[128,1024]{1,0:T(8,128)(2,1)S(1)} %get-tuple-element.18.q_in, bf16[128,1024]{1,0:T(8,128)(2,1)S(1)} %get-tuple-element.19.k_in, ...), custom_call_target="tpu_custom_call" | custom-call | tf_op jit(solution)/shard_map/pallas_call | solution.py:590
